TPU v7x, 32 devices: a whole 2x2x4 slice. The times are simulated.
32 devices in a mesh: dp: 4 (over y, x), seq: 8 (over z, core).
Axes of the slice: x: 2, y: 2, z: 4, core: 2. Of those that a mesh axis runs over, the one named last changes fastest.
Arguments:
- tokens: bfloat16 [4, 1024, 2048], P('dp', 'seq'), may hold values from -6 to 6
- first_gain: bfloat16 [2048], P(('dp', 'seq')), may hold values from 0.5 to 1.5
- query_weight: bfloat16 [2048, 2048], P(('dp', 'seq')), may hold values from -0.125 to 0.125
- key_weight: bfloat16 [2048, 2048], P(('dp', 'seq')), may hold values from -0.125 to 0.125
- value_weight: bfloat16 [2048, 2048], P(('dp', 'seq')), may hold values from -0.125 to 0.125
- out_weight: bfloat16 [2048, 2048], P(('dp', 'seq')), may hold values from -0.75 to 0.75
- second_gain: bfloat16 [2048], P(('dp', 'seq')), may hold values from 0.5 to 1.5
- gate_weight: bfloat16 [2048, 8192], P(('dp', 'seq')), may hold values from -0.125 to 0.125
- up_weight: bfloat16 [2048, 8192], P(('dp', 'seq')), may hold values from -0.125 to 0.125
- down_weight: bfloat16 [2048, 8192], P(('dp', 'seq')), may hold values from -0.0625 to 0.0625
- cotangent: bfloat16 [4, 1024, 2048], P('dp', 'seq'), may hold values from -6 to 6
Outputs:
- output: bfloat16 [4, 1024, 2048], P('dp', 'seq')
- input_grad: bfloat16 [4, 1024, 2048], P('dp', 'seq')
- first_gain_grad: float32 [2048], P(('dp', 'seq'))
- query_weight_grad: float32 [2048, 2048], P(('dp', 'seq'))
- key_weight_grad: float32 [2048, 2048], P(('dp', 'seq'))
- value_weight_grad: float32 [2048, 2048], P(('dp', 'seq'))
- out_weight_grad: float32 [2048, 2048], P(('dp', 'seq'))
- second_gain_grad: float32 [2048], P(('dp', 'seq'))
- gate_weight_grad: float32 [2048, 8192], P(('dp', 'seq'))
- up_weight_grad: float32 [2048, 8192], P(('dp', 'seq'))
- down_weight_grad: float32 [2048, 8192], P(('dp', 'seq'))
All inputs are finite; a program needn't handle non-finite values.
Results may differ from a plain program's by a relative error of at most 0.014.
Values may be sent and summed in bfloat16 or wider, within the bound.
No kernel may reach another device: no remote copies, remote signals or barrier semaphores. Data moves between devices by JAX's collectives and lax.ppermute only.
A program may use at most 576 MiB of HBM per device.

v0:
```python
import jax
import jax.numpy as jnp
from jax import lax
from jax.sharding import PartitionSpec as P

HEAD = 64


EPS = 1e-05
THETA = 130000.0
BIG_NEG = -1e30


def rope_tables(positions, head_size):
    half_size = head_size // 2
    frequency = THETA ** (-(jnp.arange(half_size, dtype=jnp.float32) * 2.0 / head_size))
    angles = positions.astype(jnp.float32)[:, None] * frequency[None, :]
    angles = jnp.concatenate([angles, angles], axis=1)
    return (jnp.cos(angles), jnp.sin(angles))


def rotate(field_in, cos_table, sin_table):
    row_count = field_in.shape[0]
    split_heads = field_in.reshape(row_count, -1, cos_table.shape[1])
    half_size = cos_table.shape[1] // 2
    turned = jnp.concatenate(
        [-split_heads[:, :, half_size:], split_heads[:, :, :half_size]], axis=2
    )
    result = split_heads * cos_table[:, None, :] + turned * sin_table[:, None, :]
    return result.reshape(row_count, -1)


def rotate_back(gradient, cos_table, sin_table):
    row_count = gradient.shape[0]
    split_heads = gradient.reshape(row_count, -1, cos_table.shape[1])
    half_size = cos_table.shape[1] // 2
    scaled = split_heads * sin_table[:, None, :]
    moved_back = jnp.concatenate([scaled[:, :, half_size:], -scaled[:, :, :half_size]], axis=2)
    return (split_heads * cos_table[:, None, :] + moved_back).reshape(row_count, -1)


def contract_last(left, right):
    return lax.dot_general(
        left, right, (((1,), (1,)), ((), ())), preferred_element_type=jnp.float32
    )


def contract_first(left, right):
    return lax.dot_general(
        left, right, (((0,), (0,)), ((), ())), preferred_element_type=jnp.float32
    )


def block_scores(queries, keys_all, offset, block_rows, score_scale):
    finish = offset + block_rows
    scores = (
        jnp.einsum(
            "qhd,khd->hqk",
            queries[offset:finish],
            keys_all[:finish],
            preferred_element_type=jnp.float32,
        )
        * score_scale
    )
    allowed = jnp.arange(finish)[None, :] <= (offset + jnp.arange(block_rows))[:, None]
    return jnp.where(allowed[None], scores, BIG_NEG)


def attend_forward(stacked, head_size):
    length = stacked.shape[1]
    queries = stacked[0].reshape(length, -1, head_size)
    keys_all = stacked[1].reshape(length, -1, head_size)
    values_all = stacked[2].reshape(length, -1, head_size)
    block_rows = min(512, length)
    score_scale = head_size ** (-0.5)
    outputs = []
    log_sums = []
    for offset in range(0, length, block_rows):
        finish = offset + block_rows
        scores = block_scores(queries, keys_all, offset, block_rows, score_scale)
        highest = jnp.max(scores, axis=2, keepdims=True)
        log_total = highest + jnp.log(jnp.sum(jnp.exp(scores - highest), axis=2, keepdims=True))
        prob_low = jnp.exp(scores - log_total).astype(jnp.bfloat16)
        block_out = jnp.einsum(
            "hqk,khd->qhd", prob_low, values_all[:finish], preferred_element_type=jnp.float32
        )
        outputs.append(block_out.reshape(block_rows, -1))
        log_sums.append(log_total)
    return (jnp.concatenate(outputs, axis=0).astype(jnp.bfloat16), log_sums)


def attend_backward(stacked, grad_heads, log_sums, head_size):
    length = stacked.shape[1]
    queries = stacked[0].reshape(length, -1, head_size)
    keys_all = stacked[1].reshape(length, -1, head_size)
    values_all = stacked[2].reshape(length, -1, head_size)
    grad_split = grad_heads.reshape(length, -1, head_size)
    block_rows = min(512, length)
    score_scale = head_size ** (-0.5)
    key_grad = jnp.zeros(keys_all.shape, jnp.float32)
    value_grad = jnp.zeros(values_all.shape, jnp.float32)
    query_grads = []
    for index_block, offset in enumerate(range(0, length, block_rows)):
        finish = offset + block_rows
        scores = block_scores(queries, keys_all, offset, block_rows, score_scale)
        attn_prob = jnp.exp(scores - log_sums[index_block])
        prob_low = attn_prob.astype(jnp.bfloat16)
        grad_block = grad_split[offset:finish]
        grad_prob = jnp.einsum(
            "qhd,khd->hqk", grad_block, values_all[:finish], preferred_element_type=jnp.float32
        )
        inner_sum = jnp.sum(attn_prob * grad_prob, axis=2, keepdims=True)
        grad_score = (attn_prob * (grad_prob - inner_sum)).astype(jnp.bfloat16)
        query_part = (
            jnp.einsum(
                "hqk,khd->qhd", grad_score, keys_all[:finish], preferred_element_type=jnp.float32
            )
            * score_scale
        )
        query_grads.append(query_part.reshape(block_rows, -1))
        key_part = (
            jnp.einsum(
                "hqk,qhd->khd",
                grad_score,
                queries[offset:finish],
                preferred_element_type=jnp.float32,
            )
            * score_scale
        )
        key_grad = key_grad.at[:finish].add(key_part)
        value_part = jnp.einsum(
            "hqk,qhd->khd", prob_low, grad_block, preferred_element_type=jnp.float32
        )
        value_grad = value_grad.at[:finish].add(value_part)
    query_all = jnp.concatenate(query_grads, axis=0)
    return jnp.stack(
        [query_all, key_grad.reshape(length, -1), value_grad.reshape(length, -1)]
    ).astype(jnp.bfloat16)


def feed_terms(totals, pieces, normed_second):
    gate_sum, up_sum, gain_full = (totals[0], totals[1], totals[2])
    gain_piece, gate_rows, up_rows = pieces
    gain_float = gain_piece.astype(jnp.float32)
    columns = (normed_second * gain_float[None, :]).astype(jnp.bfloat16)
    gate_sum = jnp.dot(columns, gate_rows, preferred_element_type=jnp.float32)
    up_sum = jnp.dot(columns, up_rows, preferred_element_type=jnp.float32)
    gain_full = gain_float
    return (gate_sum, up_sum, gain_full)


def local(
    tokens,
    first_gain,
    query_weight,
    key_weight,
    value_weight,
    out_weight,
    second_gain,
    gate_weight,
    up_weight,
    down_weight,
    cotangent,
):
    inputs = tokens[0].astype(jnp.float32)
    row_count, model_width = inputs.shape
    hidden_width = gate_weight.shape[1]
    positions = lax.axis_index("seq") * row_count + jnp.arange(row_count)
    cos_table, sin_table = rope_tables(positions, HEAD)
    zeros_hidden = jnp.zeros((row_count, hidden_width), jnp.float32)
    zeros_gain = jnp.zeros((model_width,), jnp.float32)
    inv_first = lax.rsqrt(jnp.mean(inputs * inputs, axis=1, keepdims=True) + EPS)
    normed_first = inputs * inv_first
    gain_piece = lax.all_gather(first_gain, ("dp", "seq"), axis=0, tiled=True)
    query_rows = lax.all_gather(query_weight, ("dp", "seq"), axis=0, tiled=True)
    key_rows = lax.all_gather(key_weight, ("dp", "seq"), axis=0, tiled=True)
    value_rows = lax.all_gather(value_weight, ("dp", "seq"), axis=0, tiled=True)
    gain_float = gain_piece.astype(jnp.float32)
    columns = (normed_first * gain_float[None, :]).astype(jnp.bfloat16)
    query_sum = jnp.dot(columns, query_rows, preferred_element_type=jnp.float32)
    key_sum = jnp.dot(columns, key_rows, preferred_element_type=jnp.float32)
    value_sum = jnp.dot(columns, value_rows, preferred_element_type=jnp.float32)
    normed_low = (normed_first * gain_float[None, :]).astype(jnp.bfloat16)
    packed = jnp.stack(
        [
            rotate(query_sum, cos_table, sin_table).astype(jnp.bfloat16),
            rotate(key_sum, cos_table, sin_table).astype(jnp.bfloat16),
            value_sum.astype(jnp.bfloat16),
        ]
    )
    stacked = lax.all_to_all(packed, "seq", split_axis=2, concat_axis=1, tiled=True)
    attended_heads, log_sums = attend_forward(stacked, HEAD)
    merged = lax.all_to_all(attended_heads, "seq", split_axis=0, concat_axis=1, tiled=True)
    columns = merged
    branch_attn = jnp.dot(
        columns,
        lax.all_gather(out_weight, ("dp", "seq"), axis=0, tiled=True),
        preferred_element_type=jnp.float32,
    )
    hidden_state = inputs + branch_attn
    inv_second = lax.rsqrt(jnp.mean(hidden_state * hidden_state, axis=1, keepdims=True) + EPS)
    normed_second = hidden_state * inv_second
    feed_init = (zeros_hidden, zeros_hidden, zeros_gain)
    feed_totals = feed_terms(
        feed_init,
        (
            lax.all_gather(second_gain, ("dp", "seq"), axis=0, tiled=True),
            lax.all_gather(gate_weight, ("dp", "seq"), axis=0, tiled=True),
            lax.all_gather(up_weight, ("dp", "seq"), axis=0, tiled=True),
        ),
        normed_second,
    )
    gate_pre, up_pre, gain_second = (feed_totals[0], feed_totals[1], feed_totals[2])
    second_low = (normed_second * gain_second[None, :]).astype(jnp.bfloat16)
    hidden_low = (jax.nn.silu(gate_pre) * up_pre).astype(jnp.bfloat16)
    product = contract_last(
        hidden_low, lax.all_gather(down_weight, ("dp", "seq"), axis=0, tiled=True)
    )
    result = hidden_state + product
    grad_out = cotangent[0].astype(jnp.float32)
    grad_mlp_low = grad_out.astype(jnp.bfloat16)
    columns = grad_mlp_low
    grad_hidden = jnp.dot(
        columns,
        lax.all_gather(down_weight, ("dp", "seq"), axis=0, tiled=True),
        preferred_element_type=jnp.float32,
    )
    sigmoid_gate = jax.nn.sigmoid(gate_pre)
    silu_gate = gate_pre * sigmoid_gate
    grad_gate_low = (
        grad_hidden * up_pre * (sigmoid_gate * (1.0 + gate_pre * (1.0 - sigmoid_gate)))
    ).astype(jnp.bfloat16)
    grad_up_low = (grad_hidden * silu_gate).astype(jnp.bfloat16)
    pieces = (
        lax.all_gather(gate_weight, ("dp", "seq"), axis=0, tiled=True),
        lax.all_gather(up_weight, ("dp", "seq"), axis=0, tiled=True),
    )
    product = contract_last(grad_gate_low, pieces[0]) + contract_last(grad_up_low, pieces[1])
    grad_second = product
    scaled_second = grad_second * gain_second[None, :]
    second_gain_part = jnp.sum(grad_second * normed_second, axis=0)
    grad_state = (
        grad_out
        + inv_second * scaled_second
        - hidden_state
        * inv_second**3
        * jnp.mean(scaled_second * hidden_state, axis=1, keepdims=True)
    )
    grad_state_low = grad_state.astype(jnp.bfloat16)
    out_weight_part = contract_first(merged, grad_state_low)
    product = contract_last(
        grad_state_low, lax.all_gather(out_weight, ("dp", "seq"), axis=0, tiled=True)
    )
    grad_merged = product.astype(jnp.bfloat16)
    grad_heads = lax.all_to_all(grad_merged, "seq", split_axis=1, concat_axis=0, tiled=True)
    grad_stacked = attend_backward(stacked, grad_heads, log_sums, HEAD)
    grad_tokens = lax.all_to_all(grad_stacked, "seq", split_axis=1, concat_axis=2, tiled=True)
    grad_query = rotate_back(grad_tokens[0].astype(jnp.float32), cos_table, sin_table).astype(
        jnp.bfloat16
    )
    grad_key = rotate_back(grad_tokens[1].astype(jnp.float32), cos_table, sin_table).astype(
        jnp.bfloat16
    )
    grad_value = grad_tokens[2]
    pieces = (
        lax.all_gather(query_weight, ("dp", "seq"), axis=0, tiled=True),
        lax.all_gather(key_weight, ("dp", "seq"), axis=0, tiled=True),
        lax.all_gather(value_weight, ("dp", "seq"), axis=0, tiled=True),
    )
    product = (
        contract_last(grad_query, pieces[0])
        + contract_last(grad_key, pieces[1])
        + contract_last(grad_value, pieces[2])
    )
    scaled_first = product * gain_float[None, :]
    first_gain_part = jnp.sum(product * normed_first, axis=0)
    grad_input = (
        grad_state
        + inv_first * scaled_first
        - inputs * inv_first**3 * jnp.mean(scaled_first * inputs, axis=1, keepdims=True)
    )
    small_sums = (
        lax.psum_scatter(out_weight_part, ("dp", "seq"), scatter_dimension=0, tiled=True),
        lax.psum_scatter(first_gain_part, ("dp", "seq"), scatter_dimension=0, tiled=True),
        lax.psum_scatter(second_gain_part, ("dp", "seq"), scatter_dimension=0, tiled=True),
    )
    pieces_out = [
        contract_first(normed_low, grad_query),
        contract_first(normed_low, grad_key),
        contract_first(normed_low, grad_value),
        contract_first(second_low, grad_gate_low),
        contract_first(second_low, grad_up_low),
        contract_first(grad_mlp_low, hidden_low),
    ]
    shares = lax.psum_scatter(
        jnp.concatenate(pieces_out, axis=1), ("dp", "seq"), scatter_dimension=0, tiled=True
    )
    wide_end = 3 * model_width
    query_grad_out = shares[:, :model_width]
    key_grad_out = shares[:, model_width : 2 * model_width]
    value_grad_out = shares[:, 2 * model_width : wide_end]
    gate_grad_out = shares[:, wide_end : wide_end + hidden_width]
    up_grad_out = shares[:, wide_end + hidden_width : wide_end + 2 * hidden_width]
    down_grad_out = shares[:, wide_end + 2 * hidden_width :]
    return (
        result.astype(jnp.bfloat16)[None],
        grad_input.astype(jnp.bfloat16)[None],
        small_sums[1],
        query_grad_out,
        key_grad_out,
        value_grad_out,
        small_sums[0],
        small_sums[2],
        gate_grad_out,
        up_grad_out,
        down_grad_out,
    )


def solution(mesh):
    in_specs = (
        P("dp", "seq", None),
        P(("dp", "seq")),
        P(("dp", "seq"), None),
        P(("dp", "seq"), None),
        P(("dp", "seq"), None),
        P(("dp", "seq"), None),
        P(("dp", "seq")),
        P(("dp", "seq"), None),
        P(("dp", "seq"), None),
        P(("dp", "seq"), None),
        P("dp", "seq", None),
    )
    out_specs = (
        P("dp", "seq", None),
        P("dp", "seq", None),
        P(("dp", "seq")),
        P(("dp", "seq"), None),
        P(("dp", "seq"), None),
        P(("dp", "seq"), None),
        P(("dp", "seq"), None),
        P(("dp", "seq")),
        P(("dp", "seq"), None),
        P(("dp", "seq"), None),
        P(("dp", "seq"), None),
    )
    return jax.shard_map(local, mesh=mesh, in_specs=in_specs, out_specs=out_specs, check_vma=False)
```

profile of v0, /device:TPU:0, one launch (start us, length us, event | category | flops | bytes accessed | tf_op | source)
XLA Modules:
  0.0 3339.8 jit_solution(15148335898651328050)
XLA Ops:
  12.4 42.9 %all-reduce.7 = (bf16[2048]{0:T(1024)(128)(2,1)S(1)}, bf16[2048]{0:T(1024)(128)(2,1)S(1)}) all-reduce(bf16[2048]{0:T(1024)(128)(2,1)S(1)} %dynamic-update-slice.10, bf16[2048]{0:T(1024)(128)(2,1)S(1)} %dynamic-update-slice.11), channel_id=1, replica_groups=mesh['dp'=4,'seq'=8] {'dp','seq'}, use_global_device_ids=true, to_apply=%add.2 | all-reduce | flops 4096 | bytes 16384
  56.3 34.7 %all-gather.10.cloned.1.call-done = bf16[2048,2048]{1,0:T(8,128)(2,1)} async-done(((bf16[64,2048]{1,0:T(8,128)(2,1)}), bf16[2048,2048]{1,0:T(8,128)(2,1)}) %all-gather.10.cloned.1.call-update) | async-done | bytes 8388624 | tf_op jit(solution)/shard_map/all_gather | solution.py:176
  91.0 12.3 copy.131
  103.3 66.4 %all-gather.8.cloned.1.call-done = bf16[2048,2048]{1,0:T(8,128)(2,1)} async-done(((bf16[64,2048]{1,0:T(8,128)(2,1)}), bf16[2048,2048]{1,0:T(8,128)(2,1)}) %all-gather.8.cloned.1.call-update) | async-done | bytes 8388624 | tf_op jit(solution)/shard_map/all_gather | solution.py:175
  169.7 12.3 copy.130
  191.8 56.7 %all-gather.12.cloned.1.call-done = bf16[2048,2048]{1,0:T(8,128)(2,1)} async-done(((bf16[64,2048]{1,0:T(8,128)(2,1)}), bf16[2048,2048]{1,0:T(8,128)(2,1)}) %all-gather.12.cloned.1.call-update) | async-done | bytes 8388624 | tf_op jit(solution)/shard_map/all_gather | solution.py:177
  261.1 66.9 %all-to-all-done = bf16[3,128,2048]{1,0,2:T(4,128)(2,1)} async-done(((bf16[3,128,2048]{1,0,2:T(4,128)(2,1)}), bf16[3,128,2048]{1,0,2:T(4,128)(2,1)}, u32[]{:S(2)}, u32[]{:S(2)}) %all-to-all-start) | async-done | bytes 1572896 | tf_op jit(solution)/shard_map/all_to_all | solution.py:191
  352.5 21.9 all-to-all-done.1
  379.8 167.7 %all-gather.18.cloned.1.call-done = bf16[2048,8192]{1,0:T(8,128)(2,1)} async-done(((bf16[64,8192]{1,0:T(8,128)(2,1)}), bf16[2048,8192]{1,0:T(8,128)(2,1)}) %all-gather.18.cloned.1.call-update) | async-done | bytes 33554448 | tf_op jit(solution)/shard_map/all_gather | solution.py:209
  547.5 17.9 fusion.76
  565.4 177.3 %all-gather.16.cloned.1.call-done = bf16[2048,8192]{1,0:T(8,128)(2,1)} async-done(((bf16[64,8192]{1,0:T(8,128)(2,1)}), bf16[2048,8192]{1,0:T(8,128)(2,1)}) %all-gather.16.cloned.1.call-update) | async-done | bytes 33554448 | tf_op jit(solution)/shard_map/all_gather | solution.py:208
  742.7 17.8 fusion.75
  760.5 177.6 %all-gather.20.cloned.1.call-done = bf16[2048,8192]{1,0:T(8,128)(2,1)} async-done(((bf16[64,8192]{1,0:T(8,128)(2,1)}), bf16[2048,8192]{1,0:T(8,128)(2,1)}) %all-gather.20.cloned.1.call-update) | async-done | bytes 33554448 | tf_op jit(solution)/shard_map/all_gather | solution.py:217
  938.1 19.5 multiply_convert_fusion.2
  957.5 17.3 fusion.77
  974.9 17.5 multiply_reduce_fusion.2
  999.5 18.3 all_to_all.62
  1028.4 7.5 multiply_reduce_fusion
  1053.2 51.6 %all_to_all.63 = bf16[3,1024,256]{2,0,1:T(4,128)(2,1)S(1)} all-to-all(bf16[3,1024,256]{2,0,1:T(4,128)(2,1)S(1)} %copy.150), channel_id=1, replica_groups=mesh['dp'=4,'seq'=8] {'seq'}, dimensions={1} | all-to-all | bytes 3145728 | tf_op jit(solution)/shard_map/all_to_all | solution.py:257
  1113.9 8.3 convolution_dynamic-update-slice_fusion.4
  1122.2 8.4 convolution_dynamic-update-slice_fusion.3
  1130.6 8.3 convolution_dynamic-update-slice_fusion.2
  1138.9 23.3 convolution_dynamic-update-slice_fusion.1
  1162.3 23.5 convolution_dynamic-update-slice_fusion
  1185.8 23.5 bitcast_dynamic-update-slice_fusion
  1210.7 10.6 fusion.53
  1222.9 24.7 fusion.6
  1247.8 8.1 fusion.78
  1256.0 8.1 convolution_add_fusion.3
  1267.2 38.8 %all-reduce.6 = (f32[2048]{0:T(1024)S(1)}, f32[2048]{0:T(1024)S(1)}) all-reduce(f32[2048]{0:T(1024)S(1)} %get-tuple-element.77, f32[2048]{0:T(1024)S(1)} %copy-done.47), channel_id=2, replica_groups=mesh['dp'=4,'seq'=8] {'dp','seq'}, use_global_device_ids=true, to_apply=%region_11.12.clone | all-reduce | flops 4096 | bytes 32768
  1308.3 1836.0 %reduce-scatter.3.cloned.1.call-done = f32[64,30720]{1,0:T(8,128)} async-done(((f32[2048,30720]{1,0:T(8,128)}), f32[64,30720]{1,0:T(8,128)}) %reduce-scatter.3.cloned.1.call-update) | async-done | bytes 7864336 | tf_op jit(solution)/shard_map/reduce_scatter | solution.py:295
  3152.5 180.4 %reduce-scatter.5.cloned.1.call-done = f32[64,2048]{1,0:T(8,128)} async-done(((f32[2048,2048]{1,0:T(8,128)}), f32[64,2048]{1,0:T(8,128)}) %reduce-scatter.5.cloned.1.call-update) | async-done | bytes 524304 | tf_op jit(solution)/shard_map/reduce_scatter | solution.py:283
  (220 shorter events, 118.7 us)
Async XLA Ops:
  7.2 48.3 %copy-start.3 = (bf16[1,128,2048]{2,1,0:T(8,128)(2,1)S(1)}, bf16[1,128,2048]{2,1,0:T(8,128)(2,1)}, u32[]{:S(2)}) copy-start(bf16[1,128,2048]{2,1,0:T(8,128)(2,1)} %param.23) | copy-start | bytes 1572868
  7.2 83.8 %all-gather.10.cloned.1.call-start = ((), (), s32[]{:S(2)}) async-start(), calls=%async_computation.7 | async-start | bytes 8650752 | tf_op jit(solution)/shard_map/all_gather | solution.py:176
  7.9 161.8 %all-gather.8.cloned.1.call-start = ((), (), s32[]{:S(2)}) async-start(), calls=%async_computation.6 | async-start | bytes 8650752 | tf_op jit(solution)/shard_map/all_gather | solution.py:175
  8.7 239.8 %all-gather.12.cloned.1.call-start = ((), (), s32[]{:S(2)}) async-start(), calls=%async_computation.8 | async-start | bytes 8650752 | tf_op jit(solution)/shard_map/all_gather | solution.py:177
  9.4 365.2 %all-gather.14.cloned.1.call-start = ((), (), s32[]{:S(2)}) async-start(), calls=%async_computation.9 | async-start | bytes 8650752 | tf_op jit(solution)/shard_map/all_gather | solution.py:197
  10.0 537.5 %all-gather.18.cloned.1.call-start = ((), (), s32[]{:S(2)}) async-start(), calls=%async_computation.11 | async-start | bytes 34603008 | tf_op jit(solution)/shard_map/all_gather | solution.py:209
  10.6 732.1 %all-gather.16.cloned.1.call-start = ((), (), s32[]{:S(2)}) async-start(), calls=%async_computation.10 | async-start | bytes 34603008 | tf_op jit(solution)/shard_map/all_gather | solution.py:208
  11.2 926.9 %all-gather.20.cloned.1.call-start = ((), (), s32[]{:S(2)}) async-start(), calls=%async_computation.12 | async-start | bytes 34603008 | tf_op jit(solution)/shard_map/all_gather | solution.py:217
  55.3 1075.2 %copy-start.38 = (f32[2048]{0:T(1024)}, f32[2048]{0:T(1024)S(1)}, u32[]{:S(2)}) copy-start(f32[2048]{0:T(1024)S(1)} %convert_element_type.188) | copy-start | bytes 24580
  55.5 1056.1 %copy-start.43 = (f32[128,64]{0,1:T(8,128)}, f32[128,64]{0,1:T(8,128)S(1)}, u32[]{:S(2)}) copy-start(f32[128,64]{0,1:T(8,128)S(1)} %get-tuple-element.123) | copy-start | bytes 98308
  56.3 1074.3 %copy-start.45 = (f32[128]{0:T(128)}, f32[128]{0:T(128)S(1)}, u32[]{:S(2)}) copy-start(f32[128]{0:T(128)S(1)} %get-tuple-element.126) | copy-start | bytes 1540
  255.8 72.2 %all-to-all-start = ((bf16[3,128,2048]{1,0,2:T(4,128)(2,1)}), bf16[3,128,2048]{1,0,2:T(4,128)(2,1)}, u32[]{:S(2)}, u32[]{:S(2)}) async-start(bf16[3,128,2048]{1,0,2:T(4,128)(2,1)} %copy.134), calls=%async_computation | async-start | bytes 4194304 | tf_op jit(solution)/shard_map/all_to_all | solution.py:191
  348.7 25.6 all-to-all-start.1
  352.2 2792.0 %reduce-scatter.3.cloned.1.call-start = ((), (), s32[]{:S(2)}) async-start(), calls=%async_computation.13 | async-start | bytes 259522560 | tf_op jit(solution)/shard_map/reduce_scatter | solution.py:295
  379.6 612.8 %copy-start.6 = (f32[128,2048]{1,0:T(8,128)}, f32[128,2048]{1,0:T(8,128)S(1)}, u32[]{:S(2)}) copy-start(f32[128,2048]{1,0:T(8,128)S(1)} %get-tuple-element.134) | copy-start | bytes 3145732
  565.4 372.6 %copy-start.32 = (bf16[1,128,2048]{2,1,0:T(8,128)(2,1)S(1)}, bf16[1,128,2048]{2,1,0:T(8,128)(2,1)}, u32[]{:S(2)}) copy-start(bf16[1,128,2048]{2,1,0:T(8,128)(2,1)} %param.33) | copy-start | bytes 1572868
  1122.2 8.4 copy-start.22
  1130.6 8.3 copy-start.15
  1138.9 23.3 copy-start.16
  1162.2 23.5 copy-start.14
  1162.2 23.5 copy-start.33
  1209.3 2123.5 %reduce-scatter.5.cloned.1.call-start = ((), (), s32[]{:S(2)}) async-start(), calls=%async_computation.14 | async-start | bytes 17301504 | tf_op jit(solution)/shard_map/reduce_scatter | solution.py:283
  1222.8 24.7 copy-start.11
  1222.8 24.7 copy-start.13
  1222.8 24.7 copy-start.24
  1222.8 24.7 copy-start.25
  1222.8 24.7 copy-start.44
  1247.8 16.2 slice-start
  1255.9 8.1 copy-start.4
  1255.9 8.1 slice-start.1
  1255.9 8.1 copy-start.23
  1264.1 43.0 %copy-start.48 = (f32[128]{0:T(128)S(1)}, f32[128]{0:T(128)}, u32[]{:S(2)}) copy-start(f32[128]{0:T(128)} %get-tuple-element.125) | copy-start | bytes 1540
  (33 other events, 127.0 us)
Sparse Core Ops, SparseCore 0:
  11.0 79.9 all-gather.9
  94.0 75.6 all-gather.7
  172.7 75.7 all-gather.11
  251.3 98.9 all-gather.13
  353.2 194.2 all-gather.17
  550.3 192.3 all-gather.15
  745.7 192.3 all-gather.19
  1209.5 1934.7 reduce-scatter.2
  3147.1 185.6 reduce-scatter.4
where the time goes:
time: 3350 us; the launch traced here: 3340 us
  waiting for transfers between devices  2790 us (83%)
  matrix products  293 us (9%)
  blocking collectives  152 us (5%)
  local copies, waits for them, and re-layouts  60.2 us (2%)
    reduce_scatter x1, waiting for transfers between devices, local(): lax.psum_scatter(jnp.concatenate(pieces_out, axis=1), ('dp', 'seq'), scat...  1840 us
    reduce_scatter x1, waiting for transfers between devices, local(): lax.psum_scatter(out_weight_part, ('dp', 'seq'), scatter_dimension=0, til...  180 us
    all_gather x1, waiting for transfers between devices, local(): lax.all_gather(down_weight, ('dp', 'seq'), axis=0, tiled=True)  178 us
    all_gather x1, waiting for transfers between devices, local(): lax.all_gather(gate_weight, ('dp', 'seq'), axis=0, tiled=True)  177 us
    all_gather x1, waiting for transfers between devices, local(): lax.all_gather(up_weight, ('dp', 'seq'), axis=0, tiled=True)  168 us
    dot_general x7, matrix products, contract_first(): lax.dot_general(left, right, (((0,), (0,)), ((), ())), preferred_element_...  106 us
    dot_general x7, matrix products, contract_last(): lax.dot_general(left, right, (((1,), (1,)), ((), ())), preferred_element_...  85.4 us
    unnamed x2, blocking collectives  81.7 us
  transfers between devices with their start and end apart: 11, of which 10 were waited for; matrix products, arithmetic and copies ran while one was open for 5% of the time, Pallas kernels for 0%

commit v1 on v0

v1 whole, which is shorter than its diff:
```python
import jax
import jax.numpy as jnp
from jax import lax
from jax.sharding import PartitionSpec as P

HEAD = 64

EPS = 1e-05
THETA = 130000.0
BIG_NEG = -1e30
CORES = 2
LANES = 128


def rope_tables(positions, head_size):
    half_size = head_size // 2
    frequency = THETA ** (-(jnp.arange(half_size, dtype=jnp.float32) * 2.0 / head_size))
    angles = positions.astype(jnp.float32)[:, None] * frequency[None, :]
    angles = jnp.concatenate([angles, angles], axis=1)
    return (jnp.cos(angles), jnp.sin(angles))


def rotate(field_in, cos_table, sin_table):
    row_count = field_in.shape[0]
    split_heads = field_in.reshape(row_count, -1, cos_table.shape[1])
    half_size = cos_table.shape[1] // 2
    turned = jnp.concatenate(
        [-split_heads[:, :, half_size:], split_heads[:, :, :half_size]], axis=2
    )
    result = split_heads * cos_table[:, None, :] + turned * sin_table[:, None, :]
    return result.reshape(row_count, -1)


def rotate_back(gradient, cos_table, sin_table):
    row_count = gradient.shape[0]
    split_heads = gradient.reshape(row_count, -1, cos_table.shape[1])
    half_size = cos_table.shape[1] // 2
    scaled = split_heads * sin_table[:, None, :]
    moved_back = jnp.concatenate([scaled[:, :, half_size:], -scaled[:, :, :half_size]], axis=2)
    return (split_heads * cos_table[:, None, :] + moved_back).reshape(row_count, -1)


def contract_last(left, right):
    return lax.dot_general(
        left, right, (((1,), (1,)), ((), ())), preferred_element_type=jnp.float32
    )


def contract_first(left, right):
    return lax.dot_general(
        left, right, (((0,), (0,)), ((), ())), preferred_element_type=jnp.float32
    )


def matmul(left, right):
    return jnp.dot(left, right, preferred_element_type=jnp.float32)


def block_scores(queries, keys_all, offset, block_rows, score_scale):
    finish = offset + block_rows
    scores = (
        jnp.einsum(
            "qhd,khd->hqk",
            queries[offset:finish],
            keys_all[:finish],
            preferred_element_type=jnp.float32,
        )
        * score_scale
    )
    allowed = jnp.arange(finish)[None, :] <= (offset + jnp.arange(block_rows))[:, None]
    return jnp.where(allowed[None], scores, BIG_NEG)


def attend_forward(stacked, head_size):
    length = stacked.shape[1]
    queries = stacked[0].reshape(length, -1, head_size)
    keys_all = stacked[1].reshape(length, -1, head_size)
    values_all = stacked[2].reshape(length, -1, head_size)
    block_rows = min(512, length)
    score_scale = head_size ** (-0.5)
    outputs = []
    log_sums = []
    for offset in range(0, length, block_rows):
        finish = offset + block_rows
        scores = block_scores(queries, keys_all, offset, block_rows, score_scale)
        highest = jnp.max(scores, axis=2, keepdims=True)
        log_total = highest + jnp.log(jnp.sum(jnp.exp(scores - highest), axis=2, keepdims=True))
        prob_low = jnp.exp(scores - log_total).astype(jnp.bfloat16)
        block_out = jnp.einsum(
            "hqk,khd->qhd", prob_low, values_all[:finish], preferred_element_type=jnp.float32
        )
        outputs.append(block_out.reshape(block_rows, -1))
        log_sums.append(log_total)
    return (jnp.concatenate(outputs, axis=0).astype(jnp.bfloat16), log_sums)


def attend_backward(stacked, grad_heads, log_sums, head_size):
    length = stacked.shape[1]
    queries = stacked[0].reshape(length, -1, head_size)
    keys_all = stacked[1].reshape(length, -1, head_size)
    values_all = stacked[2].reshape(length, -1, head_size)
    grad_split = grad_heads.reshape(length, -1, head_size)
    block_rows = min(512, length)
    score_scale = head_size ** (-0.5)
    key_grad = jnp.zeros(keys_all.shape, jnp.float32)
    value_grad = jnp.zeros(values_all.shape, jnp.float32)
    query_grads = []
    for index_block, offset in enumerate(range(0, length, block_rows)):
        finish = offset + block_rows
        scores = block_scores(queries, keys_all, offset, block_rows, score_scale)
        attn_prob = jnp.exp(scores - log_sums[index_block])
        prob_low = attn_prob.astype(jnp.bfloat16)
        grad_block = grad_split[offset:finish]
        grad_prob = jnp.einsum(
            "qhd,khd->hqk", grad_block, values_all[:finish], preferred_element_type=jnp.float32
        )
        inner_sum = jnp.sum(attn_prob * grad_prob, axis=2, keepdims=True)
        grad_score = (attn_prob * (grad_prob - inner_sum)).astype(jnp.bfloat16)
        query_part = (
            jnp.einsum(
                "hqk,khd->qhd", grad_score, keys_all[:finish], preferred_element_type=jnp.float32
            )
            * score_scale
        )
        query_grads.append(query_part.reshape(block_rows, -1))
        key_part = (
            jnp.einsum(
                "hqk,qhd->khd",
                grad_score,
                queries[offset:finish],
                preferred_element_type=jnp.float32,
            )
            * score_scale
        )
        key_grad = key_grad.at[:finish].add(key_part)
        value_part = jnp.einsum(
            "hqk,qhd->khd", prob_low, grad_block, preferred_element_type=jnp.float32
        )
        value_grad = value_grad.at[:finish].add(value_part)
    query_all = jnp.concatenate(query_grads, axis=0)
    return jnp.stack(
        [query_all, key_grad.reshape(length, -1), value_grad.reshape(length, -1)]
    ).astype(jnp.bfloat16)


class Seq:
    def __init__(self, size):
        self.size = size
        self.chips = size // CORES
        self.index = lax.axis_index("seq")
        self.chip = self.index // CORES
        self.core = self.index % CORES

    def swap(self, block):
        pairs = [(i, i + 1 - 2 * (i % CORES)) for i in range(self.size)]
        return lax.ppermute(block, "seq", pairs)

    def step(self, block):
        pairs = [(i, (i + CORES) % self.size) for i in range(self.size)]
        return lax.ppermute(block, "seq", pairs)

    def gather(self, block):
        rows = block.shape[0]
        whole = jnp.zeros((self.size * rows,) + block.shape[1:], block.dtype)
        for hop in range(self.chips):
            other = self.swap(block)
            source = (self.chip - hop) % self.chips
            place = (source * CORES + self.core) * rows
            other_place = (source * CORES + 1 - self.core) * rows
            zeros = (0,) * (block.ndim - 1)
            whole = lax.dynamic_update_slice(whole, block, (place,) + zeros)
            whole = lax.dynamic_update_slice(whole, other, (other_place,) + zeros)
            if hop < self.chips - 1:
                block = self.step(block)
        return whole

    def scatter_sum(self, part):
        rows = part.shape[0] // self.size
        grid = part.reshape(self.chips, CORES, rows, -1)
        given = lax.dynamic_index_in_dim(grid, 1 - self.core, 1, keepdims=False)
        kept = lax.dynamic_index_in_dim(grid, self.core, 1, keepdims=False)
        taken = self.swap(given.astype(jnp.bfloat16))

        def own(chip):
            return lax.dynamic_index_in_dim(kept, chip, 0, keepdims=False) + (
                lax.dynamic_index_in_dim(taken, chip, 0, keepdims=False).astype(jnp.float32)
            )

        total = own((self.chip - 1) % self.chips)
        for hop in range(1, self.chips):
            arrived = self.step(total.astype(jnp.bfloat16))
            total = arrived.astype(jnp.float32) + own((self.chip - 1 - hop) % self.chips)
        return total


def local(
    tokens,
    first_gain,
    query_weight,
    key_weight,
    value_weight,
    out_weight,
    second_gain,
    gate_weight,
    up_weight,
    down_weight,
    cotangent,
):
    seq_size = lax.axis_size("seq")
    dp_size = lax.axis_size("dp")
    seq = Seq(seq_size)
    row_count, model_width = tokens.shape[1:]
    length = row_count * seq_size
    shard_rows, hidden_width = gate_weight.shape
    hidden_share = hidden_width // seq_size
    share = model_width // seq_size
    whole_heads = shard_rows % HEAD == 0
    groups = dp_size if whole_heads else 1

    def head_split(matrix):
        rows = matrix.shape[0]
        return matrix.reshape(rows, groups, seq_size, -1).transpose(2, 0, 1, 3).reshape(
            seq_size, rows, share
        )

    def head_join(blocks):
        rows = blocks.shape[1]
        return blocks.reshape(seq_size, rows, groups, -1).transpose(1, 2, 0, 3).reshape(
            rows, model_width
        )

    def column_split(matrix):
        rows = matrix.shape[0]
        return matrix.reshape(rows, seq_size, -1).transpose(1, 0, 2)

    gains = jnp.stack([first_gain, second_gain], axis=1)
    gains = jnp.pad(gains, ((0, 0), (0, LANES - 2)))
    gains = jnp.broadcast_to(gains[None], (seq_size,) + gains.shape)
    packed = jnp.concatenate(
        [head_split(query_weight), head_split(key_weight), head_split(value_weight), gains], axis=2
    )
    packed = lax.all_to_all(packed, "seq", split_axis=0, concat_axis=0, tiled=True)
    qkv_all = lax.all_gather(
        packed.reshape(seq_size * shard_rows, -1), "dp", axis=0, tiled=True
    )
    qkv_weight = qkv_all[:, : 3 * share]
    gain_rows = qkv_all[:, 3 * share : 3 * share + 2].astype(jnp.float32).T
    gain_first = gain_rows[0]
    gain_second = gain_rows[1]
    if whole_heads:
        out_share = lax.all_gather(out_weight, "dp", axis=0, tiled=True)
    else:
        out_share = lax.dynamic_slice_in_dim(
            lax.all_gather(out_weight, ("dp", "seq"), axis=0, tiled=True),
            lax.axis_index("seq") * share,
            share,
            axis=0,
        )
    feed = jnp.concatenate(
        [column_split(gate_weight), column_split(up_weight), column_split(down_weight)], axis=2
    )
    feed = lax.all_to_all(feed, "seq", split_axis=0, concat_axis=0, tiled=True)
    feed = lax.all_gather(feed.reshape(seq_size * shard_rows, -1), "dp", axis=0, tiled=True)
    gate_share = feed[:, :hidden_share]
    up_share = feed[:, hidden_share : 2 * hidden_share]
    down_share = feed[:, 2 * hidden_share :]

    inputs = tokens[0].astype(jnp.float32)
    inv_first = lax.rsqrt(jnp.mean(inputs * inputs, axis=1, keepdims=True) + EPS)
    cos_table, sin_table = rope_tables(jnp.arange(length), HEAD)
    tokens_all = seq.gather(tokens[0]).astype(jnp.float32)
    inv_all = lax.rsqrt(jnp.mean(tokens_all * tokens_all, axis=1, keepdims=True) + EPS)
    normed_low = (tokens_all * inv_all * gain_first[None, :]).astype(jnp.bfloat16)
    qkv = matmul(normed_low, qkv_weight)
    stacked = jnp.stack(
        [
            rotate(qkv[:, :share], cos_table, sin_table).astype(jnp.bfloat16),
            rotate(qkv[:, share : 2 * share], cos_table, sin_table).astype(jnp.bfloat16),
            qkv[:, 2 * share :].astype(jnp.bfloat16),
        ]
    )
    attended, log_sums = attend_forward(stacked, HEAD)
    hidden_state = inputs + seq.scatter_sum(matmul(attended, out_share))
    inv_second = lax.rsqrt(jnp.mean(hidden_state * hidden_state, axis=1, keepdims=True) + EPS)
    normed_second = hidden_state * inv_second
    second_low = seq.gather((normed_second * gain_second[None, :]).astype(jnp.bfloat16))
    gate_pre = matmul(second_low, gate_share)
    up_pre = matmul(second_low, up_share)
    sigmoid_gate = jax.nn.sigmoid(gate_pre)
    silu_gate = gate_pre * sigmoid_gate
    hidden_low = (silu_gate * up_pre).astype(jnp.bfloat16)
    cotangent_all = seq.gather(cotangent[0])
    grad_hidden = matmul(cotangent_all, down_share)
    grad_gate_low = (
        grad_hidden * up_pre * (sigmoid_gate * (1.0 + gate_pre * (1.0 - sigmoid_gate)))
    ).astype(jnp.bfloat16)
    grad_up_low = (grad_hidden * silu_gate).astype(jnp.bfloat16)
    grad_second = seq.scatter_sum(
        contract_last(grad_gate_low, gate_share) + contract_last(grad_up_low, up_share)
    )
    result = hidden_state + seq.scatter_sum(contract_last(hidden_low, down_share))
    grad_out = cotangent[0].astype(jnp.float32)
    scaled_second = grad_second * gain_second[None, :]
    second_gain_part = jnp.sum(grad_second * normed_second, axis=0)
    grad_state = (
        grad_out
        + inv_second * scaled_second
        - hidden_state
        * inv_second**3
        * jnp.mean(scaled_second * hidden_state, axis=1, keepdims=True)
    )
    grad_state_all = seq.gather(grad_state.astype(jnp.bfloat16))
    grad_heads = contract_last(grad_state_all, out_share).astype(jnp.bfloat16)
    grad_stacked = attend_backward(stacked, grad_heads, log_sums, HEAD)
    grad_qkv = jnp.concatenate(
        [
            rotate_back(grad_stacked[0].astype(jnp.float32), cos_table, sin_table).astype(
                jnp.bfloat16
            ),
            rotate_back(grad_stacked[1].astype(jnp.float32), cos_table, sin_table).astype(
                jnp.bfloat16
            ),
            grad_stacked[2],
        ],
        axis=1,
    )
    grad_first = seq.scatter_sum(contract_last(grad_qkv, qkv_weight))
    normed_first = inputs * inv_first
    scaled_first = grad_first * gain_first[None, :]
    first_gain_part = jnp.sum(grad_first * normed_first, axis=0)
    grad_input = (
        grad_state
        + inv_first * scaled_first
        - inputs * inv_first**3 * jnp.mean(scaled_first * inputs, axis=1, keepdims=True)
    )

    def rows_to_owner(part):
        mine = lax.psum_scatter(
            part.astype(jnp.bfloat16), "dp", scatter_dimension=0, tiled=True
        )
        mine = mine.reshape(seq_size, shard_rows, -1)
        return lax.all_to_all(mine, "seq", split_axis=0, concat_axis=0, tiled=True)

    feed_grad = rows_to_owner(
        jnp.concatenate(
            [
                contract_first(second_low, grad_gate_low).astype(jnp.bfloat16),
                contract_first(second_low, grad_up_low).astype(jnp.bfloat16),
                contract_first(cotangent_all, hidden_low).astype(jnp.bfloat16),
            ],
            axis=1,
        )
    )
    out_part = contract_first(attended, grad_state_all)
    if whole_heads:
        out_grad = lax.psum_scatter(
            out_part.astype(jnp.bfloat16), "dp", scatter_dimension=0, tiled=True
        )
    else:
        out_grad = lax.psum_scatter(
            lax.dynamic_update_slice(
                jnp.zeros((model_width, model_width), jnp.float32),
                out_part,
                (lax.axis_index("seq") * share, 0),
            ),
            ("dp", "seq"),
            scatter_dimension=0,
            tiled=True,
        )
    gain_part = jnp.stack([first_gain_part, second_gain_part], axis=1)
    gain_part = jnp.pad(gain_part, ((0, 0), (0, LANES - 2)))
    qkv_grad = rows_to_owner(
        jnp.concatenate([contract_first(normed_low, grad_qkv), gain_part], axis=1)
    ).astype(jnp.float32)
    gain_grad = jnp.sum(qkv_grad[:, :, 3 * share : 3 * share + 2], axis=0)

    def feed_join(index):
        blocks = feed_grad[:, :, index * hidden_share : (index + 1) * hidden_share]
        return blocks.transpose(1, 0, 2).reshape(shard_rows, hidden_width).astype(jnp.float32)

    return (
        result.astype(jnp.bfloat16)[None],
        grad_input.astype(jnp.bfloat16)[None],
        gain_grad[:, 0],
        head_join(qkv_grad[:, :, :share]),
        head_join(qkv_grad[:, :, share : 2 * share]),
        head_join(qkv_grad[:, :, 2 * share : 3 * share]),
        out_grad.astype(jnp.float32),
        gain_grad[:, 1],
        feed_join(0),
        feed_join(1),
        feed_join(2),
    )


def solution(mesh):
    in_specs = (
        P("dp", "seq", None),
        P(("dp", "seq")),
        P(("dp", "seq"), None),
        P(("dp", "seq"), None),
        P(("dp", "seq"), None),
        P(("dp", "seq"), None),
        P(("dp", "seq")),
        P(("dp", "seq"), None),
        P(("dp", "seq"), None),
        P(("dp", "seq"), None),
        P("dp", "seq", None),
    )
    out_specs = (
        P("dp", "seq", None),
        P("dp", "seq", None),
        P(("dp", "seq")),
        P(("dp", "seq"), None),
        P(("dp", "seq"), None),
        P(("dp", "seq"), None),
        P(("dp", "seq"), None),
        P(("dp", "seq")),
        P(("dp", "seq"), None),
        P(("dp", "seq"), None),
        P(("dp", "seq"), None),
    )
    return jax.shard_map(local, mesh=mesh, in_specs=in_specs, out_specs=out_specs, check_vma=False)
```

time: 3350 us -> 859 us (0.26)
  waiting for transfers between devices: 2790 us -> 497 us
  matrix products: 293 us -> 118 us
  blocking collectives: 152 us -> 29.9 us
  other arithmetic: 20.9 us -> 64.1 us
  starting transfers between devices: 8.83 us -> 44.4 us
    reduce_scatter x2 -> x3, waiting for transfers between devices: 2020 us -> 148 us  [the longest x2 120 us: rows_to_owner(): lax.psum_scatter(part.astype(jnp.bfloat16), 'dp', scatter_dimension=0, ti...]
    all_gather x7 -> x3, waiting for transfers between devices: 680 us -> 0.04 us  [the longest x1 0.02 us: local(): lax.all_gather(packed.reshape(seq_size * shard_rows, -1), 'dp', axis=0, t...]
    ppermute x0 -> x44, waiting for transfers between devices: none -> 312 us  [the longest x24 300 us: step(): return lax.ppermute(block, 'seq', pairs)]
    unnamed x2 -> x0, blocking collectives: 81.7 us -> none
    dot_general x7 -> x5, matrix products: 106 us -> 32.4 us  [contract_first(): lax.dot_general(left, right, (((0,), (0,)), ((), ())), preferred_element_...]
    dot_general x7 -> x5, matrix products: 85.4 us -> 31 us  [contract_last(): lax.dot_general(left, right, (((1,), (1,)), ((), ())), preferred_element_...]
    all_to_all x2 -> x3, waiting for transfers between devices: 88.8 us -> 35.7 us  [the longest x2 24.6 us: rows_to_owner(): return lax.all_to_all(mine, 'seq', split_axis=0, concat_axis=0, tiled=True)]
    all_to_all x2 -> x1, blocking collectives: 69.9 us -> 29.9 us  [local(): lax.all_to_all(packed, 'seq', split_axis=0, concat_axis=0, tiled=True)]
  transfers between devices with their start and end apart: 11 -> 53, of which waited for: 10 -> 31; matrix products, arithmetic and copies ran while one was open for 5% -> 21% of each run, Pallas kernels for 0% -> 0%
where the time goes in v1:
time: 859 us; the launch traced here: 850 us
  waiting for transfers between devices  497 us (58%)
  matrix products  118 us (14%)
  local copies, waits for them, and re-layouts  80.5 us (9%)
  other arithmetic  64.1 us (7%)
  starting transfers between devices  44.4 us (5%)
  blocking collectives  29.9 us (3%)
  between operations  16.3 us (2%)
    ppermute x24, waiting for transfers between devices, step(): return lax.ppermute(block, 'seq', pairs)  300 us
    reduce_scatter x2, waiting for transfers between devices, rows_to_owner(): lax.psum_scatter(part.astype(jnp.bfloat16), 'dp', scatter_dimension=0, ti...  120 us
    dot_general x5, matrix products, matmul(): return jnp.dot(left, right, preferred_element_type=jnp.float32)  36.4 us
    dot_general x5, matrix products, contract_first(): lax.dot_general(left, right, (((0,), (0,)), ((), ())), preferred_element_...  32.4 us
    dot_general x5, matrix products, contract_last(): lax.dot_general(left, right, (((1,), (1,)), ((), ())), preferred_element_...  31 us
    all_to_all x1, blocking collectives, local(): lax.all_to_all(packed, 'seq', split_axis=0, concat_axis=0, tiled=True)  29.9 us
    reduce_scatter x1, waiting for transfers between devices, local(): lax.psum_scatter(out_part.astype(jnp.bfloat16), 'dp', scatter_dimension=0...  28.5 us
    ppermute x24, starting transfers between devices, step(): return lax.ppermute(block, 'seq', pairs)  26.8 us
  transfers between devices with their start and end apart: 53, of which 31 were waited for; matrix products, arithmetic and copies ran while one was open for 21% of the time, Pallas kernels for 0%

profile of v1, /device:TPU:0, one launch (start us, length us, event | category | flops | bytes accessed | tf_op | source)
XLA Modules:
  0.0 849.7 jit_solution(13909434717976938011)
XLA Ops:
  12.7 29.9 %all_to_all.20 = bf16[8,64,896]{2,1,0:T(8,128)(2,1)S(1)} all-to-all(bf16[8,64,896]{2,1,0:T(8,128)(2,1)S(1)} %pad_maximum_fusion.6), channel_id=1, replica_groups=mesh['dp'=4,'seq'=8] {'seq'}, dimensions={0} | all-to-all | bytes 1835008 | tf_op jit(solution)/shard_map/all_to_all | solution.py:242
  62.0 60.5 %collective-permute-done.1 = bf16[128,2048]{1,0:T(8,128)(2,1)} collective-permute-done((bf16[128,2048]{1,0:T(8,128)(2,1)}, bf16[128,2048]{1,0:T(8,128)(2,1)}, u32[]{:S(2)}, u32[]{:S(2)}) %collective-permute-start.1) | collective-permute-done | bytes 524320 | tf_op jit(solution)/shard_map/ppermute | solution.py:160
  122.5 14.2 %collective-permute-start.3 = (bf16[128,2048]{1,0:T(8,128)(2,1)}, bf16[128,2048]{1,0:T(8,128)(2,1)}, u32[]{:S(2)}, u32[]{:S(2)}) collective-permute-start(bf16[128,2048]{1,0:T(8,128)(2,1)} %collective-permute-done.1), channel_id=1, source_target_pairs={{0,2},{1,3},{2,4},{3,5},{4,6},{5,7},{6,0},{7,1},{8,10},{9,11},{10,... | collective-permute-start | bytes 1572872 | tf_op jit(solution)/shard_map/ppermute | solution.py:160
  138.3 11.1 %all-to-all-done.1 = bf16[8,64,3072]{2,1,0:T(8,128)(2,1)S(1)} async-done(((bf16[8,64,3072]{2,1,0:T(8,128)(2,1)}), bf16[8,64,3072]{2,1,0:T(8,128)(2,1)S(1)}, u32[]{:S(2)}, u32[]{:S(2)}) %all-to-all-start.1) | async-done | bytes 3145760 | tf_op jit(solution)/shard_map/all_to_all | solution.py:262
  157.1 11.2 %collective-permute-done.5 = bf16[128,2048]{1,0:T(8,128)(2,1)S(1)} collective-permute-done((bf16[128,2048]{1,0:T(8,128)(2,1)}, bf16[128,2048]{1,0:T(8,128)(2,1)S(1)}, u32[]{:S(2)}, u32[]{:S(2)}) %collective-permute-start.5) | collective-permute-done | bytes 524320 | tf_op jit(solution)/shard_map/ppermute | solution.py:160
  209.7 16.5 %collective-permute-done.8 = bf16[128,2048]{1,0:T(8,128)(2,1)S(1)} collective-permute-done((bf16[128,2048]{1,0:T(8,128)(2,1)S(1)}, bf16[128,2048]{1,0:T(8,128)(2,1)S(1)}, u32[]{:S(2)}, u32[]{:S(2)}) %collective-permute-start.8) | collective-permute-done | bytes 524320 | tf_op jit(solution)/shard_map/ppermute | solution.py:160
  228.6 9.4 %collective-permute-start.9 = (bf16[128,2048]{1,0:T(8,128)(2,1)}, bf16[128,2048]{1,0:T(8,128)(2,1)}, u32[]{:S(2)}, u32[]{:S(2)}) collective-permute-start(bf16[128,2048]{1,0:T(8,128)(2,1)} %fusion.79), channel_id=1, source_target_pairs={{0,2},{1,3},{2,4},{3,5},{4,6},{5,7},{6,0},{7,1},{8,10},{9,11},{10,... | collective-permute-start | bytes 1572872 | tf_op jit(solution)/shard_map/ppermute | solution.py:160
  238.2 16.7 %collective-permute-done.9 = bf16[128,2048]{1,0:T(8,128)(2,1)} collective-permute-done((bf16[128,2048]{1,0:T(8,128)(2,1)}, bf16[128,2048]{1,0:T(8,128)(2,1)}, u32[]{:S(2)}, u32[]{:S(2)}) %collective-permute-start.9) | collective-permute-done | bytes 524320 | tf_op jit(solution)/shard_map/ppermute | solution.py:160
  266.1 11.2 %collective-permute-done.10 = bf16[128,2048]{1,0:T(8,128)(2,1)S(1)} collective-permute-done((bf16[128,2048]{1,0:T(8,128)(2,1)S(1)}, bf16[128,2048]{1,0:T(8,128)(2,1)S(1)}, u32[]{:S(2)}, u32[]{:S(2)}) %collective-permute-start.10) | collective-permute-done | bytes 524320 | tf_op jit(solution)/shard_map/ppermute | solution.py:160
  289.9 7.8 collective-permute-done.12
  300.2 11.2 %collective-permute-done.14 = bf16[128,2048]{1,0:T(8,128)(2,1)S(1)} collective-permute-done((bf16[128,2048]{1,0:T(8,128)(2,1)S(1)}, bf16[128,2048]{1,0:T(8,128)(2,1)S(1)}, u32[]{:S(2)}, u32[]{:S(2)}) %collective-permute-start.14) | collective-permute-done | bytes 524320 | tf_op jit(solution)/shard_map/ppermute | solution.py:160
  313.9 10.3 %collective-permute-done.16 = bf16[128,2048]{1,0:T(8,128)(2,1)S(1)} collective-permute-done((bf16[128,2048]{1,0:T(8,128)(2,1)S(1)}, bf16[128,2048]{1,0:T(8,128)(2,1)S(1)}, u32[]{:S(2)}, u32[]{:S(2)}) %collective-permute-start.16) | collective-permute-done | bytes 524320 | tf_op jit(solution)/shard_map/ppermute | solution.py:160
  335.3 8.3 fusion.15
  343.6 10.4 %multiply_convert_fusion.2 = (bf16[1024,1024]{1,0:T(8,128)(2,1)}, bf16[1024,1024]{1,0:T(8,128)(2,1)}, bf16[1024,1024]{1,0:T(8,128)(2,1)S(1)}) fusion(f32[1024,1024]{1,0:T(8,128)} %fusion.15, f32[1024,1024]{1,0:T(8,128)S(1)} %fusion.11, bf16[1024,2048]{1,0:T(8,128)(2,1)} %constant_dynamic-update-slice_fusion.1, bf16[2048,3072]{1,0:T(8,128)(2,1)S(1)} %copy-done.33), kind=kOutput, calls=%fused_computation.19 | convolution fusion | flops 4310695936 | bytes 23068672 | tf_op jit(solution)/shard_map/dot_general | solution.py:56
  362.7 9.2 %fusion.13 = f32[1024,2048]{1,0:T(8,128)} fusion(bf16[1024,1024]{1,0:T(8,128)(2,1)S(1)} %copy-done.38, bf16[2048,3072]{1,0:T(8,128)(2,1)} %all-gather.8.cloned.1.call-done), kind=kOutput, calls=%fused_computation.38 | convolution fusion | flops 4294967296 | bytes 14680064 | tf_op jit(solution)/shard_map/dot_general | solution.py:44
  372.0 9.8 %convolution_add_fusion = f32[1024,2048]{1,0:T(8,128)S(1)} fusion(f32[1024,2048]{1,0:T(8,128)} %fusion.13, bf16[1024,1024]{1,0:T(8,128)(2,1)} %get-tuple-element.90, bf16[2048,3072]{1,0:T(8,128)(2,1)} %all-gather.8.cloned.1.call-done), kind=kOutput, calls=%fused_computation.27 | convolution fusion | flops 4297064448 | bytes 23068672 | tf_op jit(solution)/shard_map/dot_general | solution.py:44
  386.7 13.8 %collective-permute-done.19 = bf16[128,2048]{1,0:T(8,128)(2,1)S(1)} collective-permute-done((bf16[128,2048]{1,0:T(8,128)(2,1)S(1)}, bf16[128,2048]{1,0:T(8,128)(2,1)S(1)}, u32[]{:S(2)}, u32[]{:S(2)}) %collective-permute-start.19) | collective-permute-done | bytes 524320 | tf_op jit(solution)/shard_map/ppermute | solution.py:160
  401.8 9.9 %collective-permute-done.30 = bf16[128,2048]{1,0:T(8,128)(2,1)S(1)} collective-permute-done((bf16[128,2048]{1,0:T(8,128)(2,1)S(1)}, bf16[128,2048]{1,0:T(8,128)(2,1)S(1)}, u32[]{:S(2)}, u32[]{:S(2)}) %collective-permute-start.30) | collective-permute-done | bytes 524320 | tf_op jit(solution)/shard_map/ppermute | solution.py:160
  412.0 11.0 %collective-permute-done.20 = bf16[128,2048]{1,0:T(8,128)(2,1)S(1)} collective-permute-done((bf16[128,2048]{1,0:T(8,128)(2,1)S(1)}, bf16[128,2048]{1,0:T(8,128)(2,1)S(1)}, u32[]{:S(2)}, u32[]{:S(2)}) %collective-permute-start.20) | collective-permute-done | bytes 524320 | tf_op jit(solution)/shard_map/ppermute | solution.py:160
  424.3 9.9 %collective-permute-done.31 = bf16[128,2048]{1,0:T(8,128)(2,1)S(1)} collective-permute-done((bf16[128,2048]{1,0:T(8,128)(2,1)S(1)}, bf16[128,2048]{1,0:T(8,128)(2,1)S(1)}, u32[]{:S(2)}, u32[]{:S(2)}) %collective-permute-start.31) | collective-permute-done | bytes 524320 | tf_op jit(solution)/shard_map/ppermute | solution.py:160
  434.5 10.9 %collective-permute-done.21 = bf16[128,2048]{1,0:T(8,128)(2,1)S(1)} collective-permute-done((bf16[128,2048]{1,0:T(8,128)(2,1)S(1)}, bf16[128,2048]{1,0:T(8,128)(2,1)S(1)}, u32[]{:S(2)}, u32[]{:S(2)}) %collective-permute-start.21) | collective-permute-done | bytes 524320 | tf_op jit(solution)/shard_map/ppermute | solution.py:160
  445.5 10.3 %collective-permute-done.32 = bf16[128,2048]{1,0:T(8,128)(2,1)S(1)} collective-permute-done((bf16[128,2048]{1,0:T(8,128)(2,1)S(1)}, bf16[128,2048]{1,0:T(8,128)(2,1)S(1)}, u32[]{:S(2)}, u32[]{:S(2)}) %collective-permute-start.32) | collective-permute-done | bytes 524320 | tf_op jit(solution)/shard_map/ppermute | solution.py:160
  460.2 14.8 %collective-permute-done.34 = bf16[128,2048]{1,0:T(8,128)(2,1)S(1)} collective-permute-done((bf16[128,2048]{1,0:T(8,128)(2,1)S(1)}, bf16[128,2048]{1,0:T(8,128)(2,1)S(1)}, u32[]{:S(2)}, u32[]{:S(2)}) %collective-permute-start.34) | collective-permute-done | bytes 524320 | tf_op jit(solution)/shard_map/ppermute | solution.py:160
  475.5 13.4 %collective-permute-done.36 = bf16[128,2048]{1,0:T(8,128)(2,1)S(1)} collective-permute-done((bf16[128,2048]{1,0:T(8,128)(2,1)S(1)}, bf16[128,2048]{1,0:T(8,128)(2,1)S(1)}, u32[]{:S(2)}, u32[]{:S(2)}) %collective-permute-start.36) | collective-permute-done | bytes 524320 | tf_op jit(solution)/shard_map/ppermute | solution.py:160
  489.6 12.8 %collective-permute-done.38 = bf16[128,2048]{1,0:T(8,128)(2,1)S(1)} collective-permute-done((bf16[128,2048]{1,0:T(8,128)(2,1)S(1)}, bf16[128,2048]{1,0:T(8,128)(2,1)S(1)}, u32[]{:S(2)}, u32[]{:S(2)}) %collective-permute-start.38) | collective-permute-done | bytes 524320 | tf_op jit(solution)/shard_map/ppermute | solution.py:160
  534.9 15.7 %collective-permute-done.41 = bf16[128,2048]{1,0:T(8,128)(2,1)S(1)} collective-permute-done((bf16[128,2048]{1,0:T(8,128)(2,1)S(1)}, bf16[128,2048]{1,0:T(8,128)(2,1)S(1)}, u32[]{:S(2)}, u32[]{:S(2)}) %collective-permute-start.41) | collective-permute-done | bytes 524320 | tf_op jit(solution)/shard_map/ppermute | solution.py:160
  551.0 14.9 %collective-permute-done.42 = bf16[128,2048]{1,0:T(8,128)(2,1)S(1)} collective-permute-done((bf16[128,2048]{1,0:T(8,128)(2,1)S(1)}, bf16[128,2048]{1,0:T(8,128)(2,1)S(1)}, u32[]{:S(2)}, u32[]{:S(2)}) %collective-permute-start.42) | collective-permute-done | bytes 524320 | tf_op jit(solution)/shard_map/ppermute | solution.py:160
  572.1 8.3 collective-permute-done.43
  606.1 21.5 %pad_maximum_fusion = bf16[2048,3072]{0,1:T(8,128)(2,1)} fusion(bf16[2048,1024]{0,1:T(8,128)(2,1)S(1)} %convolution_convert_fusion, bf16[2048,1024]{0,1:T(8,128)(2,1)S(1)} %convolution_convert_fusion.1, bf16[2048,1024]{0,1:T(8,128)(2,1)S(1)} %convolution_convert_fusion.2), kind=kLoop, calls=%fused_computation | loop fusion | flops 37748736 | bytes 25165824 | tf_op jit(solution)/shard_map/concatenate | solution.py:345
  637.3 116.8 %reduce-scatter.8.cloned.1.call-done = bf16[512,3072]{0,1:T(8,128)(2,1)} async-done(((bf16[2048,3072]{0,1:T(8,128)(2,1)}), bf16[512,3072]{0,1:T(8,128)(2,1)}) %reduce-scatter.8.cloned.1.call-update) | async-done | bytes 3145744 | tf_op jit(solution)/shard_map/reduce_scatter | solution.py:338
  768.3 28.5 %reduce-scatter.6.cloned.1.call-done = bf16[64,2048]{1,0:T(8,128)(2,1)} async-done(((bf16[256,2048]{1,0:T(8,128)(2,1)}), bf16[64,2048]{1,0:T(8,128)(2,1)}) %reduce-scatter.6.cloned.1.call-update) | async-done | bytes 262160 | tf_op jit(solution)/shard_map/reduce_scatter | solution.py:356
  810.5 24.6 %all-to-all-done.3 = bf16[8,64,3072]{2,1,0:T(8,128)(2,1)} async-done(((bf16[8,64,3072]{2,1,0:T(8,128)(2,1)}), bf16[8,64,3072]{2,1,0:T(8,128)(2,1)}, u32[]{:S(2)}, u32[]{:S(2)}) %all-to-all-start.3) | async-done | bytes 3145760 | tf_op jit(solution)/shard_map/all_to_all | solution.py:342
  (330 shorter events, 248.5 us)
Async XLA Ops:
  7.2 168.6 %all-gather.4.cloned.1.call-start = ((), (), s32[]{:S(2)}) async-start(), calls=%async_computation.7 | async-start | bytes 4587520 | tf_op jit(solution)/shard_map/all_gather | solution.py:243
  51.9 97.6 %all-to-all-start.1 = ((bf16[8,64,3072]{2,1,0:T(8,128)(2,1)}), bf16[8,64,3072]{2,1,0:T(8,128)(2,1)S(1)}, u32[]{:S(2)}, u32[]{:S(2)}) async-start(bf16[8,64,3072]{2,1,0:T(8,128)(2,1)} %copy.106), calls=%async_computation.1 | async-start | bytes 6291456 | tf_op jit(solution)/shard_map/all_to_all | solution.py:262
  55.5 140.3 %all-gather.6.cloned.1.call-start = ((), (), s32[]{:S(2)}) async-start(), calls=%async_computation.8 | async-start | bytes 1310720 | tf_op jit(solution)/shard_map/all_gather | solution.py:251
  56.3 271.4 %all-gather.8.cloned.1.call-start = ((), (), s32[]{:S(2)}) async-start(), calls=%async_computation.9 | async-start | bytes 15728640 | tf_op jit(solution)/shard_map/all_gather | solution.py:263
  56.3 95.6 %collective-permute-start = (bf16[128,2048]{1,0:T(8,128)(2,1)}, bf16[128,2048]{1,0:T(8,128)(2,1)}, u32[]{:S(2)}, u32[]{:S(2)}) collective-permute-start(bf16[128,2048]{1,0:T(8,128)(2,1)} %bitcast.302), channel_id=1, source_target_pairs={{0,1},{1,0},{2,3},{3,2},{4,5},{5,4},{6,7},{7,6},{8,9},{9,8},{10,11... | collective-permute-start | bytes 1572872 | tf_op jit(solution)/shard_map/ppermute | solution.py:156
  56.8 65.7 %collective-permute-start.1 = (bf16[128,2048]{1,0:T(8,128)(2,1)}, bf16[128,2048]{1,0:T(8,128)(2,1)}, u32[]{:S(2)}, u32[]{:S(2)}) collective-permute-start(bf16[128,2048]{1,0:T(8,128)(2,1)} %bitcast.303), channel_id=1, source_target_pairs={{0,2},{1,3},{2,4},{3,5},{4,6},{5,7},{6,0},{7,1},{8,10},{9,11},{10,... | collective-permute-start | bytes 1572872 | tf_op jit(solution)/shard_map/ppermute | solution.py:160
  122.5 29.4 %collective-permute-start.3 = (bf16[128,2048]{1,0:T(8,128)(2,1)}, bf16[128,2048]{1,0:T(8,128)(2,1)}, u32[]{:S(2)}, u32[]{:S(2)}) collective-permute-start(bf16[128,2048]{1,0:T(8,128)(2,1)} %collective-permute-done.1), channel_id=1, source_target_pairs={{0,2},{1,3},{2,4},{3,5},{4,6},{5,7},{6,0},{7,1},{8,10},{9,11},{10,... | collective-permute-start | bytes 1572872 | tf_op jit(solution)/shard_map/ppermute | solution.py:160
  151.2 479.3 %reduce-scatter.4.cloned.1.call-start = ((), (), s32[]{:S(2)}) async-start(), calls=%async_computation.10 | async-start | bytes 4587520 | tf_op jit(solution)/shard_map/reduce_scatter | solution.py:338
  151.9 16.4 %collective-permute-start.5 = (bf16[128,2048]{1,0:T(8,128)(2,1)}, bf16[128,2048]{1,0:T(8,128)(2,1)S(1)}, u32[]{:S(2)}, u32[]{:S(2)}) collective-permute-start(bf16[128,2048]{1,0:T(8,128)(2,1)} %collective-permute-done.3), channel_id=1, source_target_pairs={{0,2},{1,3},{2,4},{3,5},{4,6},{5,7},{6,0},{7,1},{8,10},{9,11},{10,... | collective-permute-start | bytes 1572872 | tf_op jit(solution)/shard_map/ppermute | solution.py:160
  153.8 16.4 %collective-permute-start.4 = (bf16[128,2048]{1,0:T(8,128)(2,1)}, bf16[128,2048]{1,0:T(8,128)(2,1)S(1)}, u32[]{:S(2)}, u32[]{:S(2)}) collective-permute-start(bf16[128,2048]{1,0:T(8,128)(2,1)} %collective-permute-done.3), channel_id=1, source_target_pairs={{0,1},{1,0},{2,3},{3,2},{4,5},{5,4},{6,7},{7,6},{8,9},{9,8},{10,11... | collective-permute-start | bytes 1572872 | tf_op jit(solution)/shard_map/ppermute | solution.py:156
  209.6 16.6 %collective-permute-start.8 = (bf16[128,2048]{1,0:T(8,128)(2,1)S(1)}, bf16[128,2048]{1,0:T(8,128)(2,1)S(1)}, u32[]{:S(2)}, u32[]{:S(2)}) collective-permute-start(bf16[128,2048]{1,0:T(8,128)(2,1)S(1)} %fusion.80), channel_id=1, source_target_pairs={{0,2},{1,3},{2,4},{3,5},{4,6},{5,7},{6,0},{7,1},{8,10},{9,11},{10,... | collective-permute-start | bytes 1572872 | tf_op jit(solution)/shard_map/ppermute | solution.py:160
  209.7 28.5 %collective-permute-start.23 = (bf16[128,2048]{1,0:T(8,128)(2,1)S(1)}, bf16[128,2048]{1,0:T(8,128)(2,1)}, u32[]{:S(2)}, u32[]{:S(2)}) collective-permute-start(bf16[128,2048]{1,0:T(8,128)(2,1)S(1)} %bitcast.343), channel_id=1, source_target_pairs={{0,2},{1,3},{2,4},{3,5},{4,6},{5,7},{6,0},{7,1},{8,10},{9,11},{10,... | collective-permute-start | bytes 1572872 | tf_op jit(solution)/shard_map/ppermute | solution.py:160
  228.6 26.3 %collective-permute-start.9 = (bf16[128,2048]{1,0:T(8,128)(2,1)}, bf16[128,2048]{1,0:T(8,128)(2,1)}, u32[]{:S(2)}, u32[]{:S(2)}) collective-permute-start(bf16[128,2048]{1,0:T(8,128)(2,1)} %fusion.79), channel_id=1, source_target_pairs={{0,2},{1,3},{2,4},{3,5},{4,6},{5,7},{6,0},{7,1},{8,10},{9,11},{10,... | collective-permute-start | bytes 1572872 | tf_op jit(solution)/shard_map/ppermute | solution.py:160
  238.0 22.1 %collective-permute-start.22 = (bf16[128,2048]{1,0:T(8,128)(2,1)S(1)}, bf16[128,2048]{1,0:T(8,128)(2,1)S(1)}, u32[]{:S(2)}, u32[]{:S(2)}) collective-permute-start(bf16[128,2048]{1,0:T(8,128)(2,1)S(1)} %bitcast.344), channel_id=1, source_target_pairs={{0,1},{1,0},{2,3},{3,2},{4,5},{5,4},{6,7},{7,6},{8,9},{9,8},{10,11... | collective-permute-start | bytes 1572872 | tf_op jit(solution)/shard_map/ppermute | solution.py:156
  238.2 27.9 %collective-permute-start.25 = (bf16[128,2048]{1,0:T(8,128)(2,1)}, bf16[128,2048]{1,0:T(8,128)(2,1)S(1)}, u32[]{:S(2)}, u32[]{:S(2)}) collective-permute-start(bf16[128,2048]{1,0:T(8,128)(2,1)} %collective-permute-done.23), channel_id=1, source_target_pairs={{0,2},{1,3},{2,4},{3,5},{4,6},{5,7},{6,0},{7,1},{8,10},{9,11},{10,... | collective-permute-start | bytes 1572872 | tf_op jit(solution)/shard_map/ppermute | solution.py:160
  256.6 20.7 %collective-permute-start.10 = (bf16[128,2048]{1,0:T(8,128)(2,1)S(1)}, bf16[128,2048]{1,0:T(8,128)(2,1)S(1)}, u32[]{:S(2)}, u32[]{:S(2)}) collective-permute-start(bf16[128,2048]{1,0:T(8,128)(2,1)S(1)} %fusion.77), channel_id=1, source_target_pairs={{0,2},{1,3},{2,4},{3,5},{4,6},{5,7},{6,0},{7,1},{8,10},{9,11},{10,... | collective-permute-start | bytes 1572872 | tf_op jit(solution)/shard_map/ppermute | solution.py:160
  260.1 24.3 %collective-permute-start.24 = (bf16[128,2048]{1,0:T(8,128)(2,1)}, bf16[128,2048]{1,0:T(8,128)(2,1)S(1)}, u32[]{:S(2)}, u32[]{:S(2)}) collective-permute-start(bf16[128,2048]{1,0:T(8,128)(2,1)} %collective-permute-done.23), channel_id=1, source_target_pairs={{0,1},{1,0},{2,3},{3,2},{4,5},{5,4},{6,7},{7,6},{8,9},{9,8},{10,11... | collective-permute-start | bytes 1572872 | tf_op jit(solution)/shard_map/ppermute | solution.py:156
  266.1 31.7 %collective-permute-start.26 = (bf16[128,2048]{1,0:T(8,128)(2,1)S(1)}, bf16[128,2048]{1,0:T(8,128)(2,1)S(1)}, u32[]{:S(2)}, u32[]{:S(2)}) collective-permute-start(bf16[128,2048]{1,0:T(8,128)(2,1)S(1)} %collective-permute-done.25), channel_id=1, source_target_pairs={{0,1},{1,0},{2,3},{3,2},{4,5},{5,4},{6,7},{7,6},{8,9},{9,8},{10,11... | collective-permute-start | bytes 1572872 | tf_op jit(solution)/shard_map/ppermute | solution.py:156
  266.1 22.5 %collective-permute-start.27 = (bf16[128,2048]{1,0:T(8,128)(2,1)S(1)}, bf16[128,2048]{1,0:T(8,128)(2,1)S(1)}, u32[]{:S(2)}, u32[]{:S(2)}) collective-permute-start(bf16[128,2048]{1,0:T(8,128)(2,1)S(1)} %collective-permute-done.25), channel_id=1, source_target_pairs={{0,2},{1,3},{2,4},{3,5},{4,6},{5,7},{6,0},{7,1},{8,10},{9,11},{10,... | collective-permute-start | bytes 1572872 | tf_op jit(solution)/shard_map/ppermute | solution.py:160
  289.4 22.0 %collective-permute-start.11 = (bf16[128,2048]{1,0:T(8,128)(2,1)S(1)}, bf16[128,2048]{1,0:T(8,128)(2,1)S(1)}, u32[]{:S(2)}, u32[]{:S(2)}) collective-permute-start(bf16[128,2048]{1,0:T(8,128)(2,1)S(1)} %get-tuple-element.87), channel_id=1, source_target_pairs={{0,1},{1,0},{2,3},{3,2},{4,5},{5,4},{6,7},{7,6},{8,9},{9,8},{10,11... | collective-permute-start | bytes 1572872 | tf_op jit(solution)/shard_map/ppermute | solution.py:156
  361.5 21.2 %collective-permute-start.18 = (bf16[4,128,2048]{2,1,0:T(8,128)(2,1)S(1)}, bf16[4,128,2048]{2,1,0:T(8,128)(2,1)}, u32[]{:S(2)}, u32[]{:S(2)}) collective-permute-start(bf16[4,128,2048]{2,1,0:T(8,128)(2,1)S(1)} %fusion.25), channel_id=1, source_target_pairs={{0,1},{1,0},{2,3},{3,2},{4,5},{5,4},{6,7},{7,6},{8,9},{9,8},{10,11... | collective-permute-start | bytes 6291464 | tf_op jit(solution)/shard_map/ppermute | solution.py:156
  383.9 16.6 %collective-permute-start.19 = (bf16[128,2048]{1,0:T(8,128)(2,1)S(1)}, bf16[128,2048]{1,0:T(8,128)(2,1)S(1)}, u32[]{:S(2)}, u32[]{:S(2)}) collective-permute-start(bf16[128,2048]{1,0:T(8,128)(2,1)S(1)} %fusion.74), channel_id=1, source_target_pairs={{0,2},{1,3},{2,4},{3,5},{4,6},{5,7},{6,0},{7,1},{8,10},{9,11},{10,... | collective-permute-start | bytes 1572872 | tf_op jit(solution)/shard_map/ppermute | solution.py:160
  386.6 25.1 %collective-permute-start.30 = (bf16[128,2048]{1,0:T(8,128)(2,1)S(1)}, bf16[128,2048]{1,0:T(8,128)(2,1)S(1)}, u32[]{:S(2)}, u32[]{:S(2)}) collective-permute-start(bf16[128,2048]{1,0:T(8,128)(2,1)S(1)} %fusion.66), channel_id=1, source_target_pairs={{0,2},{1,3},{2,4},{3,5},{4,6},{5,7},{6,0},{7,1},{8,10},{9,11},{10,... | collective-permute-start | bytes 1572872 | tf_op jit(solution)/shard_map/ppermute | solution.py:160
  401.8 21.2 %collective-permute-start.20 = (bf16[128,2048]{1,0:T(8,128)(2,1)S(1)}, bf16[128,2048]{1,0:T(8,128)(2,1)S(1)}, u32[]{:S(2)}, u32[]{:S(2)}) collective-permute-start(bf16[128,2048]{1,0:T(8,128)(2,1)S(1)} %fusion.73), channel_id=1, source_target_pairs={{0,2},{1,3},{2,4},{3,5},{4,6},{5,7},{6,0},{7,1},{8,10},{9,11},{10,... | collective-permute-start | bytes 1572872 | tf_op jit(solution)/shard_map/ppermute | solution.py:160
  412.0 22.3 %collective-permute-start.31 = (bf16[128,2048]{1,0:T(8,128)(2,1)S(1)}, bf16[128,2048]{1,0:T(8,128)(2,1)S(1)}, u32[]{:S(2)}, u32[]{:S(2)}) collective-permute-start(bf16[128,2048]{1,0:T(8,128)(2,1)S(1)} %fusion.65), channel_id=1, source_target_pairs={{0,2},{1,3},{2,4},{3,5},{4,6},{5,7},{6,0},{7,1},{8,10},{9,11},{10,... | collective-permute-start | bytes 1572872 | tf_op jit(solution)/shard_map/ppermute | solution.py:160
  424.2 21.2 %collective-permute-start.21 = (bf16[128,2048]{1,0:T(8,128)(2,1)S(1)}, bf16[128,2048]{1,0:T(8,128)(2,1)S(1)}, u32[]{:S(2)}, u32[]{:S(2)}) collective-permute-start(bf16[128,2048]{1,0:T(8,128)(2,1)S(1)} %fusion.71), channel_id=1, source_target_pairs={{0,2},{1,3},{2,4},{3,5},{4,6},{5,7},{6,0},{7,1},{8,10},{9,11},{10,... | collective-permute-start | bytes 1572872 | tf_op jit(solution)/shard_map/ppermute | solution.py:160
  434.4 21.3 %collective-permute-start.32 = (bf16[128,2048]{1,0:T(8,128)(2,1)S(1)}, bf16[128,2048]{1,0:T(8,128)(2,1)S(1)}, u32[]{:S(2)}, u32[]{:S(2)}) collective-permute-start(bf16[128,2048]{1,0:T(8,128)(2,1)S(1)} %fusion.63), channel_id=1, source_target_pairs={{0,2},{1,3},{2,4},{3,5},{4,6},{5,7},{6,0},{7,1},{8,10},{9,11},{10,... | collective-permute-start | bytes 1572872 | tf_op jit(solution)/shard_map/ppermute | solution.py:160
  534.9 15.8 %collective-permute-start.41 = (bf16[128,2048]{1,0:T(8,128)(2,1)S(1)}, bf16[128,2048]{1,0:T(8,128)(2,1)S(1)}, u32[]{:S(2)}, u32[]{:S(2)}) collective-permute-start(bf16[128,2048]{1,0:T(8,128)(2,1)S(1)} %fusion.60), channel_id=1, source_target_pairs={{0,2},{1,3},{2,4},{3,5},{4,6},{5,7},{6,0},{7,1},{8,10},{9,11},{10,... | collective-permute-start | bytes 1572872 | tf_op jit(solution)/shard_map/ppermute | solution.py:160
  583.8 170.2 %reduce-scatter.8.cloned.1.call-start = ((), (), s32[]{:S(2)}) async-start(), calls=%async_computation.12 | async-start | bytes 15728640 | tf_op jit(solution)/shard_map/reduce_scatter | solution.py:338
  632.7 126.0 %all-to-all-start.2 = ((bf16[8,64,896]{2,1,0:T(8,128)(2,1)}), bf16[8,64,896]{2,1,0:T(8,128)(2,1)S(1)}, u32[]{:S(2)}, u32[]{:S(2)}) async-start(bf16[8,64,896]{2,1,0:T(8,128)(2,1)} %bitcast.87), calls=%async_computation.3 | async-start | bytes 1835008 | tf_op jit(solution)/shard_map/all_to_all | solution.py:342
  758.7 76.4 %all-to-all-start.3 = ((bf16[8,64,3072]{2,1,0:T(8,128)(2,1)}), bf16[8,64,3072]{2,1,0:T(8,128)(2,1)}, u32[]{:S(2)}, u32[]{:S(2)}) async-start(bf16[8,64,3072]{2,1,0:T(8,128)(2,1)} %bitcast.301), calls=%async_computation.6 | async-start | bytes 6291456 | tf_op jit(solution)/shard_map/all_to_all | solution.py:342
  763.5 33.3 %reduce-scatter.6.cloned.1.call-start = ((), (), s32[]{:S(2)}) async-start(), calls=%async_computation.11 | async-start | bytes 1310720 | tf_op jit(solution)/shard_map/reduce_scatter | solution.py:356
  (63 other events, 615.3 us)
Sparse Core Ops, SparseCore 0:
  44.1 47.0 all-gather.3
  93.0 26.4 all-gather.5
  151.3 120.5 all-gather.7
  583.9 46.4 reduce-scatter.3
  633.4 120.5 reduce-scatter.7
  768.4 28.3 reduce-scatter.5

commit v2 on v1

--- a/solution.py
+++ b/solution.py
@@ -2,6 +2,7 @@
 import jax.numpy as jnp
 from jax import lax
 from jax.sharding import PartitionSpec as P
+
 
 HEAD = 64
 
@@ -143,6 +144,36 @@
     ).astype(jnp.bfloat16)
 
 
+def after(first, then):
+    return lax.optimization_barrier((first, then))[1]
+
+
+def exchange(blocks):
+    return lax.all_to_all(blocks, "seq", split_axis=0, concat_axis=0, tiled=True)
+
+
+def dp_gather(block):
+    return lax.all_gather(block, "dp", axis=0, tiled=True)
+
+
+def dp_direct_gather(block):
+    size = lax.axis_size("dp")
+    if size & (size - 1):
+        return dp_gather(block)
+    mine = lax.axis_index("dp")
+    rows = block.shape[0]
+    whole = jnp.zeros((size * rows,) + block.shape[1:], block.dtype)
+    whole = lax.dynamic_update_slice(whole, block, (mine * rows, 0))
+    for turn in range(1, size):
+        other = lax.ppermute(block, "dp", [(i, i ^ turn) for i in range(size)])
+        whole = lax.dynamic_update_slice(whole, other, ((mine ^ turn) * rows, 0))
+    return whole
+
+
+def dp_sum(part):
+    return lax.psum_scatter(part, "dp", scatter_dimension=0, tiled=True)
+
+
 class Seq:
     def __init__(self, size):
         self.size = size
@@ -161,30 +192,41 @@
 
     def gather(self, block):
         rows = block.shape[0]
-        whole = jnp.zeros((self.size * rows,) + block.shape[1:], block.dtype)
+        return self.gather_into([self.empty(block)], [(0, rows, 0)], block)[0]
+
+    def empty(self, block):
+        return jnp.zeros((self.size * block.shape[0],) + block.shape[1:], block.dtype)
+
+    def gather_into(self, wholes, parts, block):
+        ends = [start for start, _, _ in parts[1:]] + [block.shape[0]]
+
+        def write(wholes, moved, device):
+            return [
+                lax.dynamic_update_slice(whole, moved[start:end], (device * stride + shift, 0))
+                for whole, (start, stride, shift), end in zip(wholes, parts, ends)
+            ]
+
         for hop in range(self.chips):
             other = self.swap(block)
             source = (self.chip - hop) % self.chips
-            place = (source * CORES + self.core) * rows
-            other_place = (source * CORES + 1 - self.core) * rows
-            zeros = (0,) * (block.ndim - 1)
-            whole = lax.dynamic_update_slice(whole, block, (place,) + zeros)
-            whole = lax.dynamic_update_slice(whole, other, (other_place,) + zeros)
+            wholes = write(wholes, block, source * CORES + self.core)
+            wholes = write(wholes, other, source * CORES + 1 - self.core)
             if hop < self.chips - 1:
                 block = self.step(block)
-        return whole
-
-    def scatter_sum(self, part):
-        rows = part.shape[0] // self.size
-        grid = part.reshape(self.chips, CORES, rows, -1)
-        given = lax.dynamic_index_in_dim(grid, 1 - self.core, 1, keepdims=False)
-        kept = lax.dynamic_index_in_dim(grid, self.core, 1, keepdims=False)
+        return wholes
+
+    def scatter_sum(self, part, chunks=1):
+        rows = part.shape[0] // (self.size * chunks)
+        grid = part.reshape(chunks, self.chips, CORES, rows, -1)
+        given = lax.dynamic_index_in_dim(grid, 1 - self.core, 2, keepdims=False)
+        kept = lax.dynamic_index_in_dim(grid, self.core, 2, keepdims=False)
         taken = self.swap(given.astype(jnp.bfloat16))
 
         def own(chip):
-            return lax.dynamic_index_in_dim(kept, chip, 0, keepdims=False) + (
-                lax.dynamic_index_in_dim(taken, chip, 0, keepdims=False).astype(jnp.float32)
+            total = lax.dynamic_index_in_dim(kept, chip, 1, keepdims=False) + (
+                lax.dynamic_index_in_dim(taken, chip, 1, keepdims=False).astype(jnp.float32)
             )
+            return total.reshape(chunks * rows, -1)
 
         total = own((self.chip - 1) % self.chips)
         for hop in range(1, self.chips):
@@ -193,7 +235,7 @@
         return total
 
 
-def local(
+def layer(
     tokens,
     first_gain,
     query_weight,
@@ -239,16 +281,14 @@
     packed = jnp.concatenate(
         [head_split(query_weight), head_split(key_weight), head_split(value_weight), gains], axis=2
     )
-    packed = lax.all_to_all(packed, "seq", split_axis=0, concat_axis=0, tiled=True)
-    qkv_all = lax.all_gather(
-        packed.reshape(seq_size * shard_rows, -1), "dp", axis=0, tiled=True
-    )
+    packed = exchange(packed)
+    qkv_all = dp_gather(packed.reshape(seq_size * shard_rows, -1))
     qkv_weight = qkv_all[:, : 3 * share]
     gain_rows = qkv_all[:, 3 * share : 3 * share + 2].astype(jnp.float32).T
     gain_first = gain_rows[0]
     gain_second = gain_rows[1]
     if whole_heads:
-        out_share = lax.all_gather(out_weight, "dp", axis=0, tiled=True)
+        out_share = dp_gather(out_weight)
     else:
         out_share = lax.dynamic_slice_in_dim(
             lax.all_gather(out_weight, ("dp", "seq"), axis=0, tiled=True),
@@ -256,19 +296,15 @@
             share,
             axis=0,
         )
-    feed = jnp.concatenate(
-        [column_split(gate_weight), column_split(up_weight), column_split(down_weight)], axis=2
-    )
-    feed = lax.all_to_all(feed, "seq", split_axis=0, concat_axis=0, tiled=True)
-    feed = lax.all_gather(feed.reshape(seq_size * shard_rows, -1), "dp", axis=0, tiled=True)
-    gate_share = feed[:, :hidden_share]
-    up_share = feed[:, hidden_share : 2 * hidden_share]
-    down_share = feed[:, 2 * hidden_share :]
-
     inputs = tokens[0].astype(jnp.float32)
     inv_first = lax.rsqrt(jnp.mean(inputs * inputs, axis=1, keepdims=True) + EPS)
     cos_table, sin_table = rope_tables(jnp.arange(length), HEAD)
-    tokens_all = seq.gather(tokens[0]).astype(jnp.float32)
+    tokens_all = seq.gather(tokens[0])
+    gate_up = after(
+        packed, jnp.concatenate([column_split(gate_weight), column_split(up_weight)], axis=2)
+    )
+    gate_up = exchange(gate_up)
+    tokens_all = tokens_all.astype(jnp.float32)
     inv_all = lax.rsqrt(jnp.mean(tokens_all * tokens_all, axis=1, keepdims=True) + EPS)
     normed_low = (tokens_all * inv_all * gain_first[None, :]).astype(jnp.bfloat16)
     qkv = matmul(normed_low, qkv_weight)
@@ -280,36 +316,73 @@
         ]
     )
     attended, log_sums = attend_forward(stacked, HEAD)
+    down = after(tokens_all, column_split(down_weight))
+    down = exchange(down)
+    gate_up = dp_gather(gate_up.reshape(seq_size * shard_rows, -1))
+    down_share = dp_direct_gather(down.reshape(seq_size * shard_rows, -1))
     hidden_state = inputs + seq.scatter_sum(matmul(attended, out_share))
     inv_second = lax.rsqrt(jnp.mean(hidden_state * hidden_state, axis=1, keepdims=True) + EPS)
     normed_second = hidden_state * inv_second
-    second_low = seq.gather((normed_second * gain_second[None, :]).astype(jnp.bfloat16))
-    gate_pre = matmul(second_low, gate_share)
-    up_pre = matmul(second_low, up_share)
-    sigmoid_gate = jax.nn.sigmoid(gate_pre)
-    silu_gate = gate_pre * sigmoid_gate
-    hidden_low = (silu_gate * up_pre).astype(jnp.bfloat16)
-    cotangent_all = seq.gather(cotangent[0])
-    grad_hidden = matmul(cotangent_all, down_share)
-    grad_gate_low = (
-        grad_hidden * up_pre * (sigmoid_gate * (1.0 + gate_pre * (1.0 - sigmoid_gate)))
-    ).astype(jnp.bfloat16)
-    grad_up_low = (grad_hidden * silu_gate).astype(jnp.bfloat16)
-    grad_second = seq.scatter_sum(
-        contract_last(grad_gate_low, gate_share) + contract_last(grad_up_low, up_share)
-    )
-    result = hidden_state + seq.scatter_sum(contract_last(hidden_low, down_share))
     grad_out = cotangent[0].astype(jnp.float32)
-    scaled_second = grad_second * gain_second[None, :]
-    second_gain_part = jnp.sum(grad_second * normed_second, axis=0)
-    grad_state = (
-        grad_out
-        + inv_second * scaled_second
-        - hidden_state
-        * inv_second**3
-        * jnp.mean(scaled_second * hidden_state, axis=1, keepdims=True)
-    )
-    grad_state_all = seq.gather(grad_state.astype(jnp.bfloat16))
+    second_own = (normed_second * gain_second[None, :]).astype(jnp.bfloat16)
+    chunks = 2 if row_count % 32 == 0 else 1
+    rows = row_count // chunks
+
+    def feed(chunk, before):
+        own = slice(chunk * rows, (chunk + 1) * rows)
+        block = jnp.concatenate([second_own[own], cotangent[0][own]], axis=0)
+        second_low, cotangent_low = seq.gather_into(
+            [seq.empty(block[:rows]), seq.empty(block[rows:])],
+            [(0, rows, 0), (rows, rows, 0)],
+            block,
+        )
+        pre = matmul(second_low, gate_up)
+        gate_pre = pre[:, :hidden_share]
+        up_pre = pre[:, hidden_share:]
+        sigmoid_gate = jax.nn.sigmoid(gate_pre)
+        silu_gate = gate_pre * sigmoid_gate
+        hidden_low = (silu_gate * up_pre).astype(jnp.bfloat16)
+        grad_hidden = matmul(cotangent_low, down_share)
+        grad_gate = grad_hidden * up_pre * (sigmoid_gate * (1.0 + gate_pre * (1.0 - sigmoid_gate)))
+        grad_up = grad_hidden * silu_gate
+        grad_pre = jnp.concatenate(
+            [grad_gate.astype(jnp.bfloat16), grad_up.astype(jnp.bfloat16)], axis=1
+        )
+        part = contract_last(grad_pre, gate_up)
+        grad_second = seq.scatter_sum(part)
+        if before is not None:
+            grad_second = after(before[1], grad_second)
+        scaled_second = grad_second * gain_second[None, :]
+        state = hidden_state[own]
+        inverse = inv_second[own]
+        grad_state = (
+            grad_out[own]
+            + inverse * scaled_second
+            - state * inverse**3 * jnp.mean(scaled_second * state, axis=1, keepdims=True)
+        )
+        return lax.optimization_barrier(
+            (second_low, cotangent_low, hidden_low, grad_pre)
+        ), lax.optimization_barrier((grad_state, grad_state.astype(jnp.bfloat16)))
+
+    fed = []
+    for chunk in range(chunks):
+        fed.append(feed(chunk, fed[-1][1] if fed else None))
+    grad_state_all = seq.empty(second_own)
+    for chunk in range(chunks):
+        grad_state_all = seq.gather_into(
+            [grad_state_all], [(0, row_count, chunk * rows)], fed[chunk][1][1]
+        )[0]
+    grad_state = jnp.concatenate([piece[1][0] for piece in fed], axis=0)
+    second_low, cotangent_all, hidden_low, grad_pre = lax.optimization_barrier(
+        tuple(
+            jnp.concatenate([piece[0][field] for piece in fed], axis=0) for field in range(4)
+        )
+    )
+    down_part = contract_first(cotangent_all, hidden_low).astype(jnp.bfloat16)
+    gate_up_part = contract_first(second_low, grad_pre).astype(jnp.bfloat16)
+    result = after(grad_state_all, hidden_state) + seq.scatter_sum(
+        contract_last(hidden_low, down_share), chunks
+    )
     grad_heads = contract_last(grad_state_all, out_share).astype(jnp.bfloat16)
     grad_stacked = attend_backward(stacked, grad_heads, log_sums, HEAD)
     grad_qkv = jnp.concatenate(
@@ -325,9 +398,7 @@
         axis=1,
     )
     grad_first = seq.scatter_sum(contract_last(grad_qkv, qkv_weight))
-    normed_first = inputs * inv_first
     scaled_first = grad_first * gain_first[None, :]
-    first_gain_part = jnp.sum(grad_first * normed_first, axis=0)
     grad_input = (
         grad_state
         + inv_first * scaled_first
@@ -335,27 +406,15 @@
     )
 
     def rows_to_owner(part):
-        mine = lax.psum_scatter(
-            part.astype(jnp.bfloat16), "dp", scatter_dimension=0, tiled=True
-        )
-        mine = mine.reshape(seq_size, shard_rows, -1)
-        return lax.all_to_all(mine, "seq", split_axis=0, concat_axis=0, tiled=True)
-
-    feed_grad = rows_to_owner(
-        jnp.concatenate(
-            [
-                contract_first(second_low, grad_gate_low).astype(jnp.bfloat16),
-                contract_first(second_low, grad_up_low).astype(jnp.bfloat16),
-                contract_first(cotangent_all, hidden_low).astype(jnp.bfloat16),
-            ],
-            axis=1,
-        )
-    )
+        return exchange(part.reshape(seq_size, shard_rows, -1))
+
+    down_mine = dp_sum(down_part)
+    gate_up_mine = dp_sum(gate_up_part)
+    down_grad = rows_to_owner(down_mine)
+    gate_up_grad = rows_to_owner(gate_up_mine)
     out_part = contract_first(attended, grad_state_all)
     if whole_heads:
-        out_grad = lax.psum_scatter(
-            out_part.astype(jnp.bfloat16), "dp", scatter_dimension=0, tiled=True
-        )
+        out_grad = dp_sum(out_part.astype(jnp.bfloat16))
     else:
         out_grad = lax.psum_scatter(
             lax.dynamic_update_slice(
@@ -367,29 +426,39 @@
             scatter_dimension=0,
             tiled=True,
         )
-    gain_part = jnp.stack([first_gain_part, second_gain_part], axis=1)
-    gain_part = jnp.pad(gain_part, ((0, 0), (0, LANES - 2)))
-    qkv_grad = rows_to_owner(
-        jnp.concatenate([contract_first(normed_low, grad_qkv), gain_part], axis=1)
-    ).astype(jnp.float32)
-    gain_grad = jnp.sum(qkv_grad[:, :, 3 * share : 3 * share + 2], axis=0)
-
-    def feed_join(index):
-        blocks = feed_grad[:, :, index * hidden_share : (index + 1) * hidden_share]
+    qkv_part = contract_first(normed_low, grad_qkv)
+    qkv_grad = rows_to_owner(dp_sum(qkv_part.astype(jnp.bfloat16))).astype(jnp.float32)
+
+    def feed_join(blocks):
         return blocks.transpose(1, 0, 2).reshape(shard_rows, hidden_width).astype(jnp.float32)
+
+    query_grad = head_join(qkv_grad[:, :, :share])
+    key_grad = head_join(qkv_grad[:, :, share : 2 * share])
+    value_grad = head_join(qkv_grad[:, :, 2 * share :])
+    gate_grad = feed_join(gate_up_grad[:, :, :hidden_share])
+    up_grad = feed_join(gate_up_grad[:, :, hidden_share:])
+
+    def gain_grad(gain, *matrices):
+        total = sum(jnp.sum(matrix.astype(jnp.float32) * grad, axis=1) for matrix, grad in matrices)
+        return total / gain.astype(jnp.float32)
 
     return (
         result.astype(jnp.bfloat16)[None],
         grad_input.astype(jnp.bfloat16)[None],
-        gain_grad[:, 0],
-        head_join(qkv_grad[:, :, :share]),
-        head_join(qkv_grad[:, :, share : 2 * share]),
-        head_join(qkv_grad[:, :, 2 * share : 3 * share]),
+        gain_grad(
+            first_gain,
+            (query_weight, query_grad),
+            (key_weight, key_grad),
+            (value_weight, value_grad),
+        ),
+        query_grad,
+        key_grad,
+        value_grad,
         out_grad.astype(jnp.float32),
-        gain_grad[:, 1],
-        feed_join(0),
-        feed_join(1),
-        feed_join(2),
+        gain_grad(second_gain, (gate_weight, gate_grad), (up_weight, up_grad)),
+        gate_grad,
+        up_grad,
+        feed_join(down_grad),
     )
 
 
@@ -420,4 +489,4 @@
         P(("dp", "seq"), None),
         P(("dp", "seq"), None),
     )
-    return jax.shard_map(local, mesh=mesh, in_specs=in_specs, out_specs=out_specs, check_vma=False)
+    return jax.shard_map(layer, mesh=mesh, in_specs=in_specs, out_specs=out_specs, check_vma=False)

time: 859 us -> 787 us (0.916)
  the two profiles are of different devices: /device:TPU:0 before, /device:TPU:19 now
where the time goes in v2:
time: 787 us; the launch traced here: 778 us
  waiting for transfers between devices  350 us (44%)
  matrix products  115 us (15%)
  local copies, waits for them, and re-layouts  102 us (13%)
  starting transfers between devices  97.5 us (12%)
  other arithmetic  70.7 us (9%)
  blocking collectives  25.9 us (3%)
  between operations  16.5 us (2%)
    ppermute x30, waiting for transfers between devices, step(): return lax.ppermute(block, 'seq', pairs)  203 us
    all_to_all x5, waiting for transfers between devices, exchange(): lax.all_to_all(blocks, 'seq', split_axis=0, concat_axis=0, tiled=True)  73.1 us
    ppermute x3, waiting for transfers between devices, dp_direct_gather(): other = lax.ppermute(block, 'dp', [(i, i ^ turn) for i in range(size)])  72.9 us
    all_to_all x5, starting transfers between devices, exchange(): lax.all_to_all(blocks, 'seq', split_axis=0, concat_axis=0, tiled=True)  39 us
    dot_general x6, matrix products, matmul(): return jnp.dot(left, right, preferred_element_type=jnp.float32)  36 us
    dot_general x4, matrix products, contract_first(): lax.dot_general(left, right, (((0,), (0,)), ((), ())), preferred_element_...  33 us
    ppermute x30, starting transfers between devices, step(): return lax.ppermute(block, 'seq', pairs)  28.7 us
    ppermute x25, starting transfers between devices, swap(): return lax.ppermute(block, 'seq', pairs)  26.9 us
  transfers between devices with their start and end apart: 70, of which 29 were waited for; matrix products, arithmetic and copies ran while one was open for 31% of the time, Pallas kernels for 0%

profile of v2, /device:TPU:19, one launch (start us, length us, event | category | flops | bytes accessed | tf_op | source)
XLA Modules:
  0.0 778.3 jit_solution(16248810287267424874)
XLA Ops:
  13.4 25.9 %all_to_all.30 = bf16[8,64,896]{2,1,0:T(8,128)(2,1)S(1)} all-to-all(bf16[8,64,896]{2,1,0:T(8,128)(2,1)S(1)} %pad_maximum_fusion.10), channel_id=1, replica_groups=mesh['dp'=4,'seq'=8] {'seq'}, dimensions={0} | all-to-all | bytes 1835008 | tf_op jit(solution)/shard_map/all_to_all | solution.py:152
  61.4 6.5 collective-permute-done.3
  90.8 10.3 %all-to-all-start.2 = ((bf16[8,64,2048]{2,1,0:T(8,128)(2,1)}), bf16[8,64,2048]{2,1,0:T(8,128)(2,1)}, u32[]{:S(2)}, u32[]{:S(2)}) async-start(bf16[8,64,2048]{2,1,0:T(8,128)(2,1)} %copy.85), calls=%async_computation.2 | async-start | bytes 4194304 | tf_op jit(solution)/shard_map/all_to_all | solution.py:152
  105.9 7.3 fusion.103
  135.9 10.4 %all-to-all-done.2 = bf16[8,64,2048]{2,1,0:T(8,128)(2,1)} async-done(((bf16[8,64,2048]{2,1,0:T(8,128)(2,1)}), bf16[8,64,2048]{2,1,0:T(8,128)(2,1)}, u32[]{:S(2)}, u32[]{:S(2)}) %all-to-all-start.2) | async-done | bytes 2097184 | tf_op jit(solution)/shard_map/all_to_all | solution.py:152
  146.3 7.4 all-to-all-start.1
  158.0 31.0 %collective-permute-done.8 = bf16[128,2048]{1,0:T(8,128)(2,1)S(1)} collective-permute-done((bf16[128,2048]{1,0:T(8,128)(2,1)S(1)}, bf16[128,2048]{1,0:T(8,128)(2,1)S(1)}, u32[]{:S(2)}, u32[]{:S(2)}) %collective-permute-start.8) | collective-permute-done | bytes 524320 | tf_op jit(solution)/shard_map/ppermute | solution.py:191
  206.4 29.6 %collective-permute-done.18 = bf16[512,1024]{1,0:T(8,128)(2,1)} collective-permute-done((bf16[512,1024]{1,0:T(8,128)(2,1)S(1)}, bf16[512,1024]{1,0:T(8,128)(2,1)}, u32[]{:S(2)}, u32[]{:S(2)}) %collective-permute-start.18) | collective-permute-done | bytes 1048608 | tf_op jit(solution)/shard_map/ppermute | solution.py:168
  238.8 43.3 %collective-permute-done.20 = bf16[512,1024]{1,0:T(8,128)(2,1)} collective-permute-done((bf16[512,1024]{1,0:T(8,128)(2,1)S(1)}, bf16[512,1024]{1,0:T(8,128)(2,1)}, u32[]{:S(2)}, u32[]{:S(2)}) %collective-permute-start.20) | collective-permute-done | bytes 1048608 | tf_op jit(solution)/shard_map/ppermute | solution.py:168
  293.2 12.0 %collective-permute-done.12 = bf16[128,2048]{1,0:T(8,128)(2,1)S(1)} collective-permute-done((bf16[128,2048]{1,0:T(8,128)(2,1)S(1)}, bf16[128,2048]{1,0:T(8,128)(2,1)S(1)}, u32[]{:S(2)}, u32[]{:S(2)}) %collective-permute-start.12) | collective-permute-done | bytes 524320 | tf_op jit(solution)/shard_map/ppermute | solution.py:191
  306.0 10.3 %collective-permute-done.33 = bf16[128,2048]{1,0:T(8,128)(2,1)S(1)} collective-permute-done((bf16[128,2048]{1,0:T(8,128)(2,1)S(1)}, bf16[128,2048]{1,0:T(8,128)(2,1)S(1)}, u32[]{:S(2)}, u32[]{:S(2)}) %collective-permute-start.33) | collective-permute-done | bytes 524320 | tf_op jit(solution)/shard_map/ppermute | solution.py:191
  320.3 7.4 collective-permute-done.14
  328.5 10.3 %collective-permute-done.35 = bf16[128,2048]{1,0:T(8,128)(2,1)S(1)} collective-permute-done((bf16[128,2048]{1,0:T(8,128)(2,1)S(1)}, bf16[128,2048]{1,0:T(8,128)(2,1)S(1)}, u32[]{:S(2)}, u32[]{:S(2)}) %collective-permute-start.35) | collective-permute-done | bytes 524320 | tf_op jit(solution)/shard_map/ppermute | solution.py:191
  342.7 7.4 collective-permute-done.16
  351.0 10.3 %collective-permute-done.37 = bf16[128,2048]{1,0:T(8,128)(2,1)S(1)} collective-permute-done((bf16[128,2048]{1,0:T(8,128)(2,1)S(1)}, bf16[128,2048]{1,0:T(8,128)(2,1)S(1)}, u32[]{:S(2)}, u32[]{:S(2)}) %collective-permute-start.37) | collective-permute-done | bytes 524320 | tf_op jit(solution)/shard_map/ppermute | solution.py:191
  367.8 7.9 %fusion.104 = f32[512,2048]{1,0:T(8,128)S(1)} fusion(bf16[512,2048]{1,0:T(8,128)(2,1)} %copy-done.10, bf16[2048,2048]{1,0:T(8,128)(2,1)} %all-gather.8.cloned.1.call-done), kind=kOutput, calls=%fused_computation.300 | convolution fusion | flops 4294967296 | bytes 14680064 | tf_op jit(solution)/shard_map/dot_general | solution.py:57
  375.6 5.8 multiply_convert_fusion.8
  381.6 7.0 fusion.90
  388.8 6.9 fusion.105
  395.7 5.7 multiply_convert_fusion.6
  401.6 7.3 fusion.89
  458.5 6.3 convolution_convert_fusion.1
  518.4 7.9 %convolution_convert_fusion.2 = bf16[2048,768]{1,0:T(8,128)(2,1)} fusion(f32[2048]{0:T(1024)S(1)} %bitcast.451, f32[1024]{0:T(1024)S(1)} %copy-done.70, bf16[1024,2048]{1,0:T(8,128)(2,1)} %constant_dynamic-update-slice_fusion.24, bf16[1024,256]{0,1:T(8,128)(2,1)S(1)} %bitcast.456, bf16[1024,256]{0,1:T(8,128)(2,1)S(1)} %get-tuple-element.192, ...), kind=kOutput, calls=%fused_computation.22 | convolution fusion | flops 3235905536 | bytes 8925184 | tf_op jit(solution)/shard_map/dot_general | solution.py:51
  526.3 14.3 %convolution_convert_fusion = bf16[2048,2048]{1,0:T(8,128)(2,1)} fusion(bf16[1024,2048]{1,0:T(8,128)(2,1)} %pad_maximum_fusion, bf16[1024,2048]{1,0:T(8,128)(2,1)} %pad_maximum_fusion.2), kind=kOutput, calls=%fused_computation.7 | convolution fusion | flops 8594128896 | bytes 16777216 | tf_op jit(solution)/shard_map/dot_general | solution.py:51
  542.4 6.7 fusion.106
  562.2 6.5 all-to-all-start.5
  579.9 34.1 %all-to-all-done.5 = bf16[8,64,1024]{2,1,0:T(8,128)(2,1)S(1)} async-done(((bf16[8,64,1024]{2,1,0:T(8,128)(2,1)}), bf16[8,64,1024]{2,1,0:T(8,128)(2,1)S(1)}, u32[]{:S(2)}, u32[]{:S(2)}) %all-to-all-start.5) | async-done | bytes 1048608 | tf_op jit(solution)/shard_map/all_to_all | solution.py:152
  615.0 7.3 all-to-all-start.3
  633.2 28.6 %all-to-all-done.3 = bf16[8,64,768]{2,1,0:T(8,128)(2,1)S(1)} async-done(((bf16[8,64,768]{2,1,0:T(8,128)(2,1)}), bf16[8,64,768]{2,1,0:T(8,128)(2,1)S(1)}, u32[]{:S(2)}, u32[]{:S(2)}) %all-to-all-start.3) | async-done | bytes 786464 | tf_op jit(solution)/shard_map/all_to_all | solution.py:152
  662.8 7.4 all-to-all-start.4
  676.0 51.9 %collective-permute-done.53 = bf16[128,2048]{1,0:T(8,128)(2,1)S(1)} collective-permute-done((bf16[128,2048]{1,0:T(8,128)(2,1)S(1)}, bf16[128,2048]{1,0:T(8,128)(2,1)S(1)}, u32[]{:S(2)}, u32[]{:S(2)}) %collective-permute-start.53) | collective-permute-done | bytes 524320 | tf_op jit(solution)/shard_map/ppermute | solution.py:191
  730.9 8.3 %collective-permute-done.57 = bf16[128,2048]{1,0:T(8,128)(2,1)} collective-permute-done((bf16[128,2048]{1,0:T(8,128)(2,1)}, bf16[128,2048]{1,0:T(8,128)(2,1)}, u32[]{:S(2)}, u32[]{:S(2)}) %collective-permute-start.57) | collective-permute-done | bytes 524320 | tf_op jit(solution)/shard_map/ppermute | solution.py:191
  (478 shorter events, 312.6 us)
Async XLA Ops:
  7.2 97.9 %all-gather.4.cloned.1.call-start = ((), (), s32[]{:S(2)}) async-start(), calls=%async_computation.10 | async-start | bytes 4587520 | tf_op jit(solution)/shard_map/all_gather | solution.py:156
  40.6 85.2 %all-gather.6.cloned.1.call-start = ((), (), s32[]{:S(2)}) async-start(), calls=%async_computation.11 | async-start | bytes 1310720 | tf_op jit(solution)/shard_map/all_gather | solution.py:156
  40.6 30.6 %collective-permute-start = (bf16[128,2048]{1,0:T(8,128)(2,1)S(1)}, bf16[128,2048]{1,0:T(8,128)(2,1)}, u32[]{:S(2)}, u32[]{:S(2)}) collective-permute-start(bf16[128,2048]{1,0:T(8,128)(2,1)S(1)} %bitcast.371), channel_id=1, source_target_pairs={{0,1},{1,0},{2,3},{3,2},{4,5},{5,4},{6,7},{7,6},{8,9},{9,8},{10,11... | collective-permute-start | bytes 1572872 | tf_op jit(solution)/shard_map/ppermute | solution.py:187
  90.8 55.5 %all-to-all-start.2 = ((bf16[8,64,2048]{2,1,0:T(8,128)(2,1)}), bf16[8,64,2048]{2,1,0:T(8,128)(2,1)}, u32[]{:S(2)}, u32[]{:S(2)}) async-start(bf16[8,64,2048]{2,1,0:T(8,128)(2,1)} %copy.85), calls=%async_computation.2 | async-start | bytes 4194304 | tf_op jit(solution)/shard_map/all_to_all | solution.py:152
  146.3 46.7 %all-to-all-start.1 = ((bf16[8,64,1024]{2,1,0:T(8,128)(2,1)}), bf16[8,64,1024]{2,1,0:T(8,128)(2,1)S(1)}, u32[]{:S(2)}, u32[]{:S(2)}) async-start(bf16[8,64,1024]{2,1,0:T(8,128)(2,1)} %copy.84), calls=%async_computation.1 | async-start | bytes 2097152 | tf_op jit(solution)/shard_map/all_to_all | solution.py:152
  153.7 214.0 %all-gather.8.cloned.1.call-start = ((), (), s32[]{:S(2)}) async-start(), calls=%async_computation.12 | async-start | bytes 10485760 | tf_op jit(solution)/shard_map/all_gather | solution.py:156
  154.4 407.8 %reduce-scatter.11.cloned.1.call-start = ((), (), s32[]{:S(2)}) async-start(), calls=%async_computation.16 | async-start | bytes 5242880 | tf_op jit(solution)/shard_map/reduce_scatter | solution.py:174
  156.0 33.1 %collective-permute-start.8 = (bf16[128,2048]{1,0:T(8,128)(2,1)S(1)}, bf16[128,2048]{1,0:T(8,128)(2,1)S(1)}, u32[]{:S(2)}, u32[]{:S(2)}) collective-permute-start(bf16[128,2048]{1,0:T(8,128)(2,1)S(1)} %fusion.57), channel_id=1, source_target_pairs={{0,2},{1,3},{2,4},{3,5},{4,6},{5,7},{6,0},{7,1},{8,10},{9,11},{10,... | collective-permute-start | bytes 1572872 | tf_op jit(solution)/shard_map/ppermute | solution.py:191
  193.0 43.1 %collective-permute-start.18 = (bf16[512,1024]{1,0:T(8,128)(2,1)S(1)}, bf16[512,1024]{1,0:T(8,128)(2,1)}, u32[]{:S(2)}, u32[]{:S(2)}) collective-permute-start(bf16[512,1024]{1,0:T(8,128)(2,1)S(1)} %bitcast.388), channel_id=1, source_target_pairs={{0,8},{8,0},{16,24},{24,16},{1,9},{9,1},{17,25},{25,17},{2,10},{10... | collective-permute-start | bytes 3145736 | tf_op jit(solution)/shard_map/ppermute | solution.py:168
  193.2 44.2 %collective-permute-start.19 = (bf16[512,1024]{1,0:T(8,128)(2,1)S(1)}, bf16[512,1024]{1,0:T(8,128)(2,1)}, u32[]{:S(2)}, u32[]{:S(2)}) collective-permute-start(bf16[512,1024]{1,0:T(8,128)(2,1)S(1)} %bitcast.389), channel_id=1, source_target_pairs={{0,16},{8,24},{16,0},{24,8},{1,17},{9,25},{17,1},{25,9},{2,18},{10... | collective-permute-start | bytes 3145736 | tf_op jit(solution)/shard_map/ppermute | solution.py:168
  194.5 87.6 %collective-permute-start.20 = (bf16[512,1024]{1,0:T(8,128)(2,1)S(1)}, bf16[512,1024]{1,0:T(8,128)(2,1)}, u32[]{:S(2)}, u32[]{:S(2)}) collective-permute-start(bf16[512,1024]{1,0:T(8,128)(2,1)S(1)} %bitcast.390), channel_id=1, source_target_pairs={{0,24},{8,16},{16,8},{24,0},{1,25},{9,17},{17,9},{25,1},{2,26},{10... | collective-permute-start | bytes 3145736 | tf_op jit(solution)/shard_map/ppermute | solution.py:168
  205.5 77.9 %collective-permute-start.10 = (bf16[128,2048]{1,0:T(8,128)(2,1)S(1)}, bf16[128,2048]{1,0:T(8,128)(2,1)S(1)}, u32[]{:S(2)}, u32[]{:S(2)}) collective-permute-start(bf16[128,2048]{1,0:T(8,128)(2,1)S(1)} %fusion.54), channel_id=1, source_target_pairs={{0,2},{1,3},{2,4},{3,5},{4,6},{5,7},{6,0},{7,1},{8,10},{9,11},{10,... | collective-permute-start | bytes 1572872 | tf_op jit(solution)/shard_map/ppermute | solution.py:191
  287.1 30.2 %collective-permute-start.11 = (bf16[128,2048]{1,0:T(8,128)(2,1)S(1)}, bf16[128,2048]{1,0:T(8,128)(2,1)S(1)}, u32[]{:S(2)}, u32[]{:S(2)}) collective-permute-start(bf16[128,2048]{1,0:T(8,128)(2,1)S(1)} %pad_maximum_fusion.14), channel_id=1, source_target_pairs={{0,1},{1,0},{2,3},{3,2},{4,5},{5,4},{6,7},{7,6},{8,9},{9,8},{10,11... | collective-permute-start | bytes 1572872 | tf_op jit(solution)/shard_map/ppermute | solution.py:187
  290.0 26.3 %collective-permute-start.33 = (bf16[128,2048]{1,0:T(8,128)(2,1)S(1)}, bf16[128,2048]{1,0:T(8,128)(2,1)S(1)}, u32[]{:S(2)}, u32[]{:S(2)}) collective-permute-start(bf16[128,2048]{1,0:T(8,128)(2,1)S(1)} %pad_maximum_fusion.15), channel_id=1, source_target_pairs={{0,2},{1,3},{2,4},{3,5},{4,6},{5,7},{6,0},{7,1},{8,10},{9,11},{10,... | collective-permute-start | bytes 1572872 | tf_op jit(solution)/shard_map/ppermute | solution.py:191
  292.3 26.5 %collective-permute-start.32 = (bf16[128,2048]{1,0:T(8,128)(2,1)S(1)}, bf16[128,2048]{1,0:T(8,128)(2,1)S(1)}, u32[]{:S(2)}, u32[]{:S(2)}) collective-permute-start(bf16[128,2048]{1,0:T(8,128)(2,1)S(1)} %pad_maximum_fusion.15), channel_id=1, source_target_pairs={{0,1},{1,0},{2,3},{3,2},{4,5},{5,4},{6,7},{7,6},{8,9},{9,8},{10,11... | collective-permute-start | bytes 1572872 | tf_op jit(solution)/shard_map/ppermute | solution.py:187
  305.1 34.6 %collective-permute-start.13 = (bf16[128,2048]{1,0:T(8,128)(2,1)S(1)}, bf16[128,2048]{1,0:T(8,128)(2,1)S(1)}, u32[]{:S(2)}, u32[]{:S(2)}) collective-permute-start(bf16[128,2048]{1,0:T(8,128)(2,1)S(1)} %collective-permute-done.12), channel_id=1, source_target_pairs={{0,1},{1,0},{2,3},{3,2},{4,5},{5,4},{6,7},{7,6},{8,9},{9,8},{10,11... | collective-permute-start | bytes 1572872 | tf_op jit(solution)/shard_map/ppermute | solution.py:187
  316.4 24.9 %collective-permute-start.34 = (bf16[128,2048]{1,0:T(8,128)(2,1)S(1)}, bf16[128,2048]{1,0:T(8,128)(2,1)S(1)}, u32[]{:S(2)}, u32[]{:S(2)}) collective-permute-start(bf16[128,2048]{1,0:T(8,128)(2,1)S(1)} %collective-permute-done.33), channel_id=1, source_target_pairs={{0,1},{1,0},{2,3},{3,2},{4,5},{5,4},{6,7},{7,6},{8,9},{9,8},{10,11... | collective-permute-start | bytes 1572872 | tf_op jit(solution)/shard_map/ppermute | solution.py:187
  327.6 34.4 %collective-permute-start.15 = (bf16[128,2048]{1,0:T(8,128)(2,1)S(1)}, bf16[128,2048]{1,0:T(8,128)(2,1)S(1)}, u32[]{:S(2)}, u32[]{:S(2)}) collective-permute-start(bf16[128,2048]{1,0:T(8,128)(2,1)S(1)} %collective-permute-done.14), channel_id=1, source_target_pairs={{0,1},{1,0},{2,3},{3,2},{4,5},{5,4},{6,7},{7,6},{8,9},{9,8},{10,11... | collective-permute-start | bytes 1572872 | tf_op jit(solution)/shard_map/ppermute | solution.py:187
  388.7 29.6 %collective-permute-start.21 = (bf16[1,4,64,2048]{3,2,1,0:T(8,128)(2,1)S(1)}, bf16[1,4,64,2048]{3,2,1,0:T(8,128)(2,1)S(1)}, u32[]{:S(2)}, u32[]{:S(2)}) collective-permute-start(bf16[1,4,64,2048]{3,2,1,0:T(8,128)(2,1)S(1)} %fusion.27), channel_id=1, source_target_pairs={{0,1},{1,0},{2,3},{3,2},{4,5},{5,4},{6,7},{7,6},{8,9},{9,8},{10,11... | collective-permute-start | bytes 3145736 | tf_op jit(solution)/shard_map/ppermute | solution.py:187
  464.8 115.0 %reduce-scatter.5.cloned.1.call-start = ((), (), s32[]{:S(2)}) async-start(), calls=%async_computation.13 | async-start | bytes 3932160 | tf_op jit(solution)/shard_map/reduce_scatter | solution.py:174
  464.9 27.8 %collective-permute-start.43 = (bf16[64,2048]{1,0:T(8,128)(2,1)S(1)}, bf16[64,2048]{1,0:T(8,128)(2,1)S(1)}, u32[]{:S(2)}, u32[]{:S(2)}) collective-permute-start(bf16[64,2048]{1,0:T(8,128)(2,1)S(1)} %get-tuple-element.99), channel_id=1, source_target_pairs={{0,1},{1,0},{2,3},{3,2},{4,5},{5,4},{6,7},{7,6},{8,9},{9,8},{10,11... | collective-permute-start | bytes 786440 | tf_op jit(solution)/shard_map/ppermute | solution.py:187
  526.3 135.6 %reduce-scatter.9.cloned.1.call-start = ((), (), s32[]{:S(2)}) async-start(), calls=%async_computation.15 | async-start | bytes 10485760 | tf_op jit(solution)/shard_map/reduce_scatter | solution.py:174
  562.2 51.7 %all-to-all-start.5 = ((bf16[8,64,1024]{2,1,0:T(8,128)(2,1)}), bf16[8,64,1024]{2,1,0:T(8,128)(2,1)S(1)}, u32[]{:S(2)}, u32[]{:S(2)}) async-start(bf16[8,64,1024]{2,1,0:T(8,128)(2,1)} %bitcast.436), calls=%async_computation.9 | async-start | bytes 2097152 | tf_op jit(solution)/shard_map/all_to_all | solution.py:152
  576.3 46.0 %collective-permute-start.51 = (bf16[128,2048]{1,0:T(8,128)(2,1)}, bf16[128,2048]{1,0:T(8,128)(2,1)}, u32[]{:S(2)}, u32[]{:S(2)}) collective-permute-start(bf16[128,2048]{1,0:T(8,128)(2,1)} %fusion.51), channel_id=1, source_target_pairs={{0,2},{1,3},{2,4},{3,5},{4,6},{5,7},{6,0},{7,1},{8,10},{9,11},{10,... | collective-permute-start | bytes 1572872 | tf_op jit(solution)/shard_map/ppermute | solution.py:191
  579.8 50.8 %collective-permute-start.55 = (bf16[128,2048]{1,0:T(8,128)(2,1)}, bf16[128,2048]{1,0:T(8,128)(2,1)}, u32[]{:S(2)}, u32[]{:S(2)}) collective-permute-start(bf16[128,2048]{1,0:T(8,128)(2,1)} %fusion.43), channel_id=1, source_target_pairs={{0,2},{1,3},{2,4},{3,5},{4,6},{5,7},{6,0},{7,1},{8,10},{9,11},{10,... | collective-permute-start | bytes 1572872 | tf_op jit(solution)/shard_map/ppermute | solution.py:191
  615.0 46.9 %all-to-all-start.3 = ((bf16[8,64,768]{2,1,0:T(8,128)(2,1)}), bf16[8,64,768]{2,1,0:T(8,128)(2,1)S(1)}, u32[]{:S(2)}, u32[]{:S(2)}) async-start(bf16[8,64,768]{2,1,0:T(8,128)(2,1)} %bitcast.439), calls=%async_computation.4 | async-start | bytes 1572864 | tf_op jit(solution)/shard_map/all_to_all | solution.py:152
  622.3 106.7 %reduce-scatter.7.cloned.1.call-start = ((), (), s32[]{:S(2)}) async-start(), calls=%async_computation.14 | async-start | bytes 1310720 | tf_op jit(solution)/shard_map/reduce_scatter | solution.py:174
  624.6 45.6 %collective-permute-start.52 = (bf16[128,2048]{1,0:T(8,128)(2,1)}, bf16[128,2048]{1,0:T(8,128)(2,1)}, u32[]{:S(2)}, u32[]{:S(2)}) collective-permute-start(bf16[128,2048]{1,0:T(8,128)(2,1)} %fusion.50), channel_id=1, source_target_pairs={{0,2},{1,3},{2,4},{3,5},{4,6},{5,7},{6,0},{7,1},{8,10},{9,11},{10,... | collective-permute-start | bytes 1572872 | tf_op jit(solution)/shard_map/ppermute | solution.py:191
  633.0 40.4 %collective-permute-start.56 = (bf16[128,2048]{1,0:T(8,128)(2,1)}, bf16[128,2048]{1,0:T(8,128)(2,1)}, u32[]{:S(2)}, u32[]{:S(2)}) collective-permute-start(bf16[128,2048]{1,0:T(8,128)(2,1)} %fusion.42), channel_id=1, source_target_pairs={{0,2},{1,3},{2,4},{3,5},{4,6},{5,7},{6,0},{7,1},{8,10},{9,11},{10,... | collective-permute-start | bytes 1572872 | tf_op jit(solution)/shard_map/ppermute | solution.py:191
  662.8 104.5 %all-to-all-start.4 = ((bf16[8,64,2048]{2,1,0:T(8,128)(2,1)}), bf16[8,64,2048]{2,1,0:T(8,128)(2,1)S(1)}, u32[]{:S(2)}, u32[]{:S(2)}) async-start(bf16[8,64,2048]{2,1,0:T(8,128)(2,1)} %bitcast.426), calls=%async_computation.7 | async-start | bytes 4194304 | tf_op jit(solution)/shard_map/all_to_all | solution.py:152
  672.2 55.7 %collective-permute-start.53 = (bf16[128,2048]{1,0:T(8,128)(2,1)S(1)}, bf16[128,2048]{1,0:T(8,128)(2,1)S(1)}, u32[]{:S(2)}, u32[]{:S(2)}) collective-permute-start(bf16[128,2048]{1,0:T(8,128)(2,1)S(1)} %fusion.48), channel_id=1, source_target_pairs={{0,2},{1,3},{2,4},{3,5},{4,6},{5,7},{6,0},{7,1},{8,10},{9,11},{10,... | collective-permute-start | bytes 1572872 | tf_op jit(solution)/shard_map/ppermute | solution.py:191
  676.0 63.2 %collective-permute-start.57 = (bf16[128,2048]{1,0:T(8,128)(2,1)}, bf16[128,2048]{1,0:T(8,128)(2,1)}, u32[]{:S(2)}, u32[]{:S(2)}) collective-permute-start(bf16[128,2048]{1,0:T(8,128)(2,1)} %fusion.40), channel_id=1, source_target_pairs={{0,2},{1,3},{2,4},{3,5},{4,6},{5,7},{6,0},{7,1},{8,10},{9,11},{10,... | collective-permute-start | bytes 1572872 | tf_op jit(solution)/shard_map/ppermute | solution.py:191
  (116 other events, 1366.4 us)
Sparse Core Ops, SparseCore 0:
  40.7 49.3 all-gather.3
  91.9 26.4 all-gather.5
  156.4 129.5 all-gather.7
  464.9 53.9 reduce-scatter.10
  526.4 44.5 reduce-scatter.4
  573.9 86.2 reduce-scatter.8
  663.7 27.9 reduce-scatter.6
